TPU v7x, 128 devices: a whole 4x4x4 slice. The times are simulated.
128 devices in a mesh: section: 2 (over z_hi), dp: 8 (over z_lo, x), expert: 8 (over y, core).
Axes of the slice: x: 4, y: 4, z: 4 (z_hi: 2, z_lo: 2; z = z_hi * 2 + z_lo), core: 2. Of those that a mesh axis runs over, the one named last changes fastest.
Arguments:
- tokens: bfloat16 [2, 16384, 3584], P('section', ('dp', 'expert')), may hold values from -0.75 to 0.75
- routes: int32 [2, 16384, 2], P('section', ('dp', 'expert')), may hold values from 0 to 7, all different within a row; in each aligned block of 256 rows (0 to 255, 256 to 511, ..., all dimensions but the last counted through in order) at most 80 rows name the same one
- hidden_grad: bfloat16 [2, 8, 8, 640, 1024], P('section', 'dp', 'expert'), may hold values from -1.5 to 1.5
- w_gate: bfloat16 [2, 8, 3584, 1024], P('section', 'expert'), may hold values from -0.75 to 0.75
- w_up: bfloat16 [2, 8, 3584, 1024], P('section', 'expert'), may hold values from -0.75 to 0.75
Outputs:
- passed_grad: bfloat16 [2, 16384, 3584], P('section', ('dp', 'expert'))
- grad_gate: bfloat16 [2, 8, 3584, 1024], P('section', 'expert', 'dp')
- grad_up: bfloat16 [2, 8, 3584, 1024], P('section', 'expert', 'dp')
Inputs may be any that keep to these rules, and one draw needn't show every extreme that they name: `routes`: each token names 2 different experts. Among the 256 tokens of one device at most 80 name the same expert, and in every draw some device's tokens name some expert exactly 80 times.
All inputs are finite; a program needn't handle non-finite values.
Results may differ from a plain program's by a relative error of at most 0.019.
Values may be sent and summed in bfloat16 or wider, within the bound.
A program may use at most 192 MiB of HBM per device.

v0:
```python
import jax
import jax.numpy as jnp
from jax import lax
from jax.sharding import PartitionSpec as P


def from_behind(value, axis, by):
    count = lax.axis_size(axis)
    return lax.ppermute(value, axis, [(i, (i + by) % count) for i in range(count)])


def slot_numbers(route_rows, experts, capacity):
    marked = (route_rows[:, :, None] == jnp.arange(experts, dtype=jnp.int32)[None, None, :]).astype(
        jnp.int32
    )
    per_token = jnp.sum(marked, axis=1)
    earlier = jnp.cumsum(per_token, axis=0) - per_token
    within = jnp.sum(marked * earlier[:, None, :], axis=2)
    return route_rows * capacity + within


def sender_rows(token_rows, slots, slot_total):
    token_count = token_rows.shape[0]
    top_slots = slots.shape[1]
    owner = jnp.full((slot_total,), token_count, jnp.int32)
    owner = owner.at[slots.reshape(-1)].set(
        jnp.repeat(jnp.arange(token_count, dtype=jnp.int32), top_slots)
    )
    padded = jnp.concatenate(
        [token_rows, jnp.zeros((1, token_rows.shape[1]), token_rows.dtype)], axis=0
    )
    return padded[owner]


def swiglu_grads(grad_hidden, gate_pre, up_pre):
    sigmoid_gate = jax.nn.sigmoid(gate_pre)
    grad_gate_pre = grad_hidden * up_pre * sigmoid_gate * (1.0 + gate_pre * (1.0 - sigmoid_gate))
    grad_up_pre = grad_hidden * gate_pre * sigmoid_gate
    return (grad_gate_pre.astype(jnp.bfloat16), grad_up_pre.astype(jnp.bfloat16))


def shards(tokens, routes, hidden_grad, w_gate, w_up):
    experts = lax.axis_size("expert")
    slot_total = hidden_grad.shape[3]
    capacity = slot_total // experts
    width = tokens.shape[2]
    slots = slot_numbers(routes[0], experts, capacity)
    outgoing = sender_rows(tokens[0], slots, slot_total)
    received = lax.all_to_all(
        outgoing.reshape(experts, capacity, width),
        "expert",
        split_axis=0,
        concat_axis=0,
        tiled=True,
    )
    received = received.reshape(slot_total, width)
    gate_w = w_gate[0, 0]
    up_w = w_up[0, 0]
    hidden = gate_w.shape[1]
    gate_pre = jnp.dot(received, gate_w, preferred_element_type=jnp.float32)
    up_pre = jnp.dot(received, up_w, preferred_element_type=jnp.float32)
    grad_gate_pre, grad_up_pre = swiglu_grads(
        hidden_grad[0, 0, 0].astype(jnp.float32), gate_pre, up_pre
    )
    along_hidden = (((1,), (1,)), ((), ()))
    slot_grad = (
        lax.dot_general(grad_gate_pre, gate_w, along_hidden, preferred_element_type=jnp.float32)
        + lax.dot_general(grad_up_pre, up_w, along_hidden, preferred_element_type=jnp.float32)
    ).astype(jnp.bfloat16)
    returned = lax.all_to_all(
        slot_grad.reshape(experts, capacity, width),
        "expert",
        split_axis=0,
        concat_axis=0,
        tiled=True,
    )
    returned = returned.reshape(slot_total, width)
    token_grad = jnp.sum(returned[slots].astype(jnp.float32), axis=1).astype(jnp.bfloat16)
    passed_grad = from_behind(token_grad[None], "section", -1)
    both_grads = jnp.concatenate([grad_gate_pre, grad_up_pre], axis=1)
    along_slots = (((0,), (0,)), ((), ()))
    summed = lax.psum_scatter(
        lax.dot_general(
            received, both_grads, along_slots, preferred_element_type=jnp.float32
        ).astype(jnp.bfloat16),
        "dp",
        scatter_dimension=0,
        tiled=True,
    ).astype(jnp.float32)
    grad_gate = summed[:, :hidden].astype(jnp.bfloat16)[None, None]
    grad_up = summed[:, hidden:].astype(jnp.bfloat16)[None, None]
    return (passed_grad, grad_gate, grad_up)


def solution(mesh):
    placed = (
        P("section", ("dp", "expert"), None),
        P("section", ("dp", "expert"), None),
        P("section", "dp", "expert", None, None),
        P("section", "expert", None, None),
        P("section", "expert", None, None),
    )
    return jax.shard_map(
        shards,
        mesh=mesh,
        in_specs=placed,
        out_specs=(
            P("section", ("dp", "expert"), None),
            P("section", "expert", "dp", None),
            P("section", "expert", "dp", None),
        ),
        check_vma=False,
    )
```

profile of v0, /device:TPU:1, one launch (start us, length us, event | category | flops | bytes accessed | tf_op | source)
XLA Modules:
  0.0 311.1 jit_solution(1508433122816741267)
XLA Ops:
  7.2 0.0 reduce-scatter.2.cloned.1.call-start
  7.2 0.7 broadcast_multiply_fusion
  7.9 0.7 convert_reduce_fusion
  8.6 0.6 reduce-window.6
  9.2 0.2 slice_reduce_fusion
  9.4 0.1 bitcast_subtract_fusion
  9.5 0.7 select_reduce_fusion
  10.2 0.1 copy.15
  10.3 0.1 reduce_sum.36
  10.5 0.1 copy.14
  10.6 0.1 mul.55
  10.8 0.1 reshape.125
  11.0 2.4 scatter_custom_fusion
  13.4 1.6 concatenate.6
  15.1 5.1 %gather_fusion = bf16[640,3584]{1,0:T(8,128)(2,1)} fusion(bf16[257,3584]{1,0:T(8,128)(2,1)S(1)} %concatenate.6, s32[1024]{0:T(1024)S(1)} %pad_clamp_fusion.1), kind=kCustom, calls=%fused_computation | custom fusion | bytes 9177600 | tf_op jit(solution)/shard_map/gather | solution.py:32
  20.1 0.0 copy-start.1
  20.2 0.0 slice-start
  20.2 60.0 %all_to_all.10 = bf16[8,80,3584]{2,1,0:T(8,128)(2,1)S(1)} all-to-all(bf16[8,80,3584]{2,1,0:T(8,128)(2,1)} %bitcast.52), channel_id=1, replica_groups=mesh['section'=2,'dp'=8,'expert'=8] {'expert'}, dimensions={0} | all-to-all | bytes 9175040 | tf_op jit(solution)/shard_map/all_to_all | solution.py:49
  80.1 0.0 copy-done.1
  80.1 0.0 slice-start.1
  80.1 7.7 %fusion.14 = (bf16[640,1024]{1,0:T(8,128)(2,1)S(1)}, f32[640,1024]{1,0:T(8,128)S(1)}) fusion(bf16[1,1,1,640,1024]{4,3,2,1,0:T(8,128)(2,1)S(1)} %copy-done.1, bf16[640,3584]{1,0:T(8,128)(2,1)S(1)} %bitcast.54, bf16[1,1,3584,1024]{3,2,1,0:T(8,128)(2,1)} %param.8), kind=kOutput, calls=%fused_computation.19 | convolution fusion | flops 4702208000 | bytes 17170432 | tf_op jit(solution)/shard_map/dot_general | solution.py:60
  87.8 0.0 slice-done
  87.8 0.0 slice-done.1
  87.8 5.5 %fusion.12 = bf16[640,1024]{1,0:T(8,128)(2,1)S(1)} fusion(f32[640,1024]{1,0:T(8,128)S(1)} %get-tuple-element.6, bf16[640,3584]{1,0:T(8,128)(2,1)S(1)} %bitcast.55, bf16[1,1,3584,1024]{3,2,1,0:T(8,128)(2,1)S(1)} %bitcast.64, bf16[1,1,1,640,1024]{4,3,2,1,0:T(8,128)(2,1)S(1)} %copy-done.1), kind=kOutput, calls=%fused_computation.17 | convolution fusion | flops 4704829440 | bytes 17170432 | tf_op jit(solution)/shard_map/dot_general | solution.py:61
  93.3 14.7 %convolution_convert_fusion = bf16[3584,2048]{1,0:T(8,128)(2,1)} fusion(bf16[640,3584]{1,0:T(8,128)(2,1)S(1)} %bitcast.56, bf16[640,1024]{1,0:T(8,128)(2,1)S(1)} %get-tuple-element.5, bf16[640,1024]{1,0:T(8,128)(2,1)S(1)} %fusion.12), kind=kOutput, calls=%fused_computation.3 | convolution fusion | flops 9407823872 | bytes 21889024 | tf_op jit(solution)/shard_map/dot_general | solution.py:83
  108.1 0.0 reduce-scatter.2.cloned.1.call-update
  108.1 11.2 %fusion = f32[640,3584]{1,0:T(8,128)} fusion(bf16[640,1024]{1,0:T(8,128)(2,1)S(1)} %fusion.12, bf16[1,1,3584,1024]{3,2,1,0:T(8,128)(2,1)} %param.8), kind=kOutput, calls=%fused_computation.5 | convolution fusion | flops 4697620480 | bytes 17825792 | tf_op jit(solution)/shard_map/dot_general | solution.py:67
  119.3 11.1 %add_convert_fusion = bf16[640,3584]{1,0:T(8,128)(2,1)} fusion(f32[640,3584]{1,0:T(8,128)} %fusion, bf16[640,1024]{1,0:T(8,128)(2,1)S(1)} %get-tuple-element.5, bf16[1,1,3584,1024]{3,2,1,0:T(8,128)(2,1)} %param.9), kind=kOutput, calls=%fused_computation.4 | convolution fusion | flops 4702208000 | bytes 22413312 | tf_op jit(solution)/shard_map/dot_general | solution.py:68
  130.4 0.0 copy-start
  130.4 5.4 %all-to-all-start.1 = ((bf16[8,80,3584]{2,1,0:T(8,128)(2,1)}), bf16[8,80,3584]{2,1,0:T(8,128)(2,1)}, u32[]{:S(2)}, u32[]{:S(2)}) async-start(bf16[8,80,3584]{2,1,0:T(8,128)(2,1)} %bitcast.53), calls=%async_computation.1 | async-start | bytes 9175040 | tf_op jit(solution)/shard_map/all_to_all | solution.py:70
  135.8 0.0 copy-done
  135.8 0.1 copy.16
  136.0 0.1 reshape.115
  136.1 52.8 %all-to-all-done.1 = bf16[8,80,3584]{2,1,0:T(8,128)(2,1)} async-done(((bf16[8,80,3584]{2,1,0:T(8,128)(2,1)}), bf16[8,80,3584]{2,1,0:T(8,128)(2,1)}, u32[]{:S(2)}, u32[]{:S(2)}) %all-to-all-start.1) | async-done | bytes 4587552 | tf_op jit(solution)/shard_map/all_to_all | solution.py:70
  189.0 10.8 %gather_fusion.1 = bf16[512,3584]{1,0:T(8,128)(2,1)} fusion(bf16[640,3584]{1,0:T(8,128)(2,1)} %bitcast.14, s32[1024]{0:T(1024)S(1)} %pad_clamp_fusion), kind=kCustom, calls=%fused_computation.1 | custom fusion | bytes 7342080 | tf_op jit(solution)/shard_map/gather | solution.py:78
  199.8 8.1 %reshape.118 = bf16[256,2,3584]{2,1,0:T(2,128)(2,1)} reshape(bf16[512,3584]{1,0:T(8,128)(2,1)} %gather_fusion.1) | data formatting | bytes 7340032 | tf_op jit(solution)/shard_map/gather | solution.py:78
  207.9 11.3 %reduce_sum.38 = bf16[256,3584]{1,0:T(8,128)(2,1)} reduce(bf16[256,2,3584]{2,1,0:T(2,128)(2,1)} %reshape.118, bf16[]{:T(256)} %constant.7.clone.1), dimensions={1}, to_apply=%region_5.6 | reduce | flops 917504 | bytes 5505026 | tf_op jit(solution)/shard_map/reduce_sum | solution.py:78
  219.2 3.2 %collective-permute-start = (bf16[1,256,3584]{2,1,0:T(8,128)(2,1)}, bf16[1,256,3584]{2,1,0:T(8,128)(2,1)S(1)}, u32[]{:S(2)}, u32[]{:S(2)}) collective-permute-start(bf16[1,256,3584]{2,1,0:T(8,128)(2,1)} %bitcast.58), channel_id=1, source_target_pairs={{0,64},{64,0},{1,65},{65,1},{2,66},{66,2},{3,67},{67,3},{4,68},{68... | collective-permute-start | bytes 5505032 | tf_op jit(solution)/shard_map/ppermute | solution.py:9
  222.4 77.8 %collective-permute-done = bf16[1,256,3584]{2,1,0:T(8,128)(2,1)S(1)} collective-permute-done((bf16[1,256,3584]{2,1,0:T(8,128)(2,1)}, bf16[1,256,3584]{2,1,0:T(8,128)(2,1)S(1)}, u32[]{:S(2)}, u32[]{:S(2)}) %collective-permute-start) | collective-permute-done | bytes 1835040 | tf_op jit(solution)/shard_map/ppermute | solution.py:9
  300.2 0.0 reduce-scatter.2.cloned.1.call-done
  300.2 2.8 slice_bitcast_fusion
  303.0 1.2 copy.18
  (9 shorter events, 0.1 us)
Async XLA Ops:
  7.2 293.0 %reduce-scatter.2.cloned.1.call-start = ((), (), s32[]{:S(2)}) async-start(), calls=%async_computation.3 | async-start | bytes 16515072 | tf_op jit(solution)/shard_map/reduce_scatter | solution.py:82
  20.1 60.0 %copy-start.1 = (bf16[1,1,1,640,1024]{4,3,2,1,0:T(8,128)(2,1)S(1)}, bf16[1,1,1,640,1024]{4,3,2,1,0:T(8,128)(2,1)}, u32[]{:S(2)}) copy-start(bf16[1,1,1,640,1024]{4,3,2,1,0:T(8,128)(2,1)} %param.7) | copy-start | bytes 3932164
  20.2 67.6 %slice-start = ((s8[7340032]{0:T(1024)(128)(4,1)}), s8[4194304]{0:T(1024)(128)(4,1)S(1)}, s32[]{:S(2)}) async-start(s8[7340032]{0:T(1024)(128)(4,1)} %bitcast.63), calls=%async_computation.4 | async-start | bytes 8388608
  80.1 7.7 %slice-start.1 = ((s8[7340032]{0:T(1024)(128)(4,1)}), s8[3145728]{0:T(1024)(128)(4,1)S(1)}, s32[]{:S(2)}) async-start(s8[7340032]{0:T(1024)(128)(4,1)} %bitcast.63), calls=%async_computation.5 | async-start | bytes 6291456
  130.4 5.4 %copy-start = (s32[1,256,2]{1,2,0:T(2,128)S(1)}, s32[1,256,2]{1,2,0:T(2,128)}, u32[]{:S(2)}) copy-start(s32[1,256,2]{1,2,0:T(2,128)} %param.6) | copy-start | bytes 6148
  130.4 58.6 %all-to-all-start.1 = ((bf16[8,80,3584]{2,1,0:T(8,128)(2,1)}), bf16[8,80,3584]{2,1,0:T(8,128)(2,1)}, u32[]{:S(2)}, u32[]{:S(2)}) async-start(bf16[8,80,3584]{2,1,0:T(8,128)(2,1)} %bitcast.53), calls=%async_computation.1 | async-start | bytes 9175040 | tf_op jit(solution)/shard_map/all_to_all | solution.py:70
  219.2 81.0 %collective-permute-start = (bf16[1,256,3584]{2,1,0:T(8,128)(2,1)}, bf16[1,256,3584]{2,1,0:T(8,128)(2,1)S(1)}, u32[]{:S(2)}, u32[]{:S(2)}) collective-permute-start(bf16[1,256,3584]{2,1,0:T(8,128)(2,1)} %bitcast.58), channel_id=1, source_target_pairs={{0,64},{64,0},{1,65},{65,1},{2,66},{66,2},{3,67},{67,3},{4,68},{68... | collective-permute-start | bytes 5505032 | tf_op jit(solution)/shard_map/ppermute | solution.py:9
Sparse Core Ops, SparseCore 0:
  108.2 152.7 reduce-scatter.1
where the time goes:
time: 312 us; the launch traced here: 311 us
  waiting for transfers between devices  131 us (42%)
  blocking collectives  60 us (19%)
  matrix products  50.2 us (16%)
  local copies, waits for them, and re-layouts  33.4 us (11%)
  between operations  14.2 us (5%)
  other arithmetic  14.1 us (5%)
  starting transfers between devices  8.7 us (3%)
    ppermute x1, waiting for transfers between devices, from_behind(): lax.ppermute(value, axis, [(i, (i + by) % count) for i in range(count)])  77.8 us
    all_to_all x1, blocking collectives, shards(): lax.all_to_all(outgoing.reshape(experts, capacity, width), 'expert', spli...  60 us
    all_to_all x1, waiting for transfers between devices, shards(): lax.all_to_all(slot_grad.reshape(experts, capacity, width), 'expert', spl...  52.8 us
    gather x2, local copies, waits for them, and re-layouts, shards(): returned[slots].astype(jnp.float32)  19 us
    dot_general x1, matrix products, shards(): lax.dot_general(received, both_grads, along_slots, preferred_element_type...  14.7 us
    reduce_sum x1, other arithmetic, shards(): jnp.sum(returned[slots].astype(jnp.float32), axis=1).astype(jnp.bfloat16)  11.3 us
    dot_general x1, matrix products, shards(): lax.dot_general(grad_gate_pre, gate_w, along_hidden, preferred_element_ty...  11.2 us
    dot_general x1, matrix products, shards(): lax.dot_general(grad_up_pre, up_w, along_hidden, preferred_element_type=j...  11.1 us
  transfers between devices with their start and end apart: 3, of which 2 were waited for; matrix products, arithmetic and copies ran while one was open for 17% of the time, Pallas kernels for 0%

commit v1 on v0

--- a/solution.py
+++ b/solution.py
@@ -19,17 +19,9 @@
     return route_rows * capacity + within
 
 
-def sender_rows(token_rows, slots, slot_total):
-    token_count = token_rows.shape[0]
-    top_slots = slots.shape[1]
-    owner = jnp.full((slot_total,), token_count, jnp.int32)
-    owner = owner.at[slots.reshape(-1)].set(
-        jnp.repeat(jnp.arange(token_count, dtype=jnp.int32), top_slots)
-    )
-    padded = jnp.concatenate(
-        [token_rows, jnp.zeros((1, token_rows.shape[1]), token_rows.dtype)], axis=0
-    )
-    return padded[owner]
+def slot_owner(slots, slot_total):
+    hit = slots[None, :, :] == jnp.arange(slot_total, dtype=jnp.int32)[:, None, None]
+    return jnp.any(hit, axis=2).astype(jnp.bfloat16)
 
 
 def swiglu_grads(grad_hidden, gate_pre, up_pre):
@@ -45,7 +37,8 @@
     capacity = slot_total // experts
     width = tokens.shape[2]
     slots = slot_numbers(routes[0], experts, capacity)
-    outgoing = sender_rows(tokens[0], slots, slot_total)
+    owner = slot_owner(slots, slot_total)
+    outgoing = jnp.dot(owner, tokens[0], preferred_element_type=jnp.float32).astype(jnp.bfloat16)
     received = lax.all_to_all(
         outgoing.reshape(experts, capacity, width),
         "expert",
@@ -62,21 +55,6 @@
     grad_gate_pre, grad_up_pre = swiglu_grads(
         hidden_grad[0, 0, 0].astype(jnp.float32), gate_pre, up_pre
     )
-    along_hidden = (((1,), (1,)), ((), ()))
-    slot_grad = (
-        lax.dot_general(grad_gate_pre, gate_w, along_hidden, preferred_element_type=jnp.float32)
-        + lax.dot_general(grad_up_pre, up_w, along_hidden, preferred_element_type=jnp.float32)
-    ).astype(jnp.bfloat16)
-    returned = lax.all_to_all(
-        slot_grad.reshape(experts, capacity, width),
-        "expert",
-        split_axis=0,
-        concat_axis=0,
-        tiled=True,
-    )
-    returned = returned.reshape(slot_total, width)
-    token_grad = jnp.sum(returned[slots].astype(jnp.float32), axis=1).astype(jnp.bfloat16)
-    passed_grad = from_behind(token_grad[None], "section", -1)
     both_grads = jnp.concatenate([grad_gate_pre, grad_up_pre], axis=1)
     along_slots = (((0,), (0,)), ((), ()))
     summed = lax.psum_scatter(
@@ -89,6 +67,30 @@
     ).astype(jnp.float32)
     grad_gate = summed[:, :hidden].astype(jnp.bfloat16)[None, None]
     grad_up = summed[:, hidden:].astype(jnp.bfloat16)[None, None]
+
+    gather_back = owner.T
+    along_hidden = (((1,), (1,)), ((), ()))
+    pieces = 4
+    step = width // pieces
+    passed = []
+    for piece in range(pieces):
+        cols = slice(piece * step, (piece + 1) * step)
+        slot_grad = (
+            lax.dot_general(grad_gate_pre, gate_w[cols], along_hidden, preferred_element_type=jnp.float32)
+            + lax.dot_general(grad_up_pre, up_w[cols], along_hidden, preferred_element_type=jnp.float32)
+        ).astype(jnp.bfloat16)
+        returned = lax.all_to_all(
+            slot_grad.reshape(experts, capacity, step),
+            "expert",
+            split_axis=0,
+            concat_axis=0,
+            tiled=True,
+        ).reshape(slot_total, step)
+        token_grad = jnp.dot(gather_back, returned, preferred_element_type=jnp.float32).astype(
+            jnp.bfloat16
+        )
+        passed.append(from_behind(token_grad, "section", -1))
+    passed_grad = jnp.concatenate(passed, axis=1)[None]
     return (passed_grad, grad_gate, grad_up)
 
 

time: 312 us -> 305 us (0.978)
  local copies, waits for them, and re-layouts: 33.4 us -> 4.14 us
  starting transfers between devices: 8.7 us -> 29.3 us
  matrix products: 50.2 us -> 64.6 us
  other arithmetic: 14.1 us -> 5.62 us
  waiting for transfers between devices: 131 us -> 127 us
    gather x3 -> x0, local copies, waits for them, and re-layouts: 24 us -> none  [the longest x2 19 us: shards(): returned[slots].astype(jnp.float32)]
    all_to_all x1 -> x4, waiting for transfers between devices: 52.8 us -> 31.8 us  [shards(): lax.all_to_all(slot_grad.reshape(experts, capacity, step), 'expert', spli...]
    ppermute x1 -> x4, waiting for transfers between devices: 77.8 us -> 95.3 us  [from_behind(): lax.ppermute(value, axis, [(i, (i + by) % count) for i in range(count)])]
    dot_general x2 -> x13, matrix products: 22.3 us -> 37.1 us  [the longest x4 16.5 us: shards(): lax.dot_general(grad_gate_pre, gate_w[cols], along_hidden, preferred_elem...]
    all_to_all x1 -> x4, starting transfers between devices: 5.44 us -> 18.5 us  [shards(): lax.all_to_all(slot_grad.reshape(experts, capacity, step), 'expert', spli...]
    reduce_sum x1 -> x0, other arithmetic: 11.3 us -> none  [shards(): jnp.sum(returned[slots].astype(jnp.float32), axis=1).astype(jnp.bfloat16)]
    ppermute x1 -> x4, starting transfers between devices: 3.22 us -> 10.7 us  [from_behind(): lax.ppermute(value, axis, [(i, (i + by) % count) for i in range(count)])]
  transfers between devices with their start and end apart: 3 -> 9, of which waited for: 2 -> 8; matrix products, arithmetic and copies ran while one was open for 17% -> 13% of each run, Pallas kernels for 0% -> 0%
where the time goes in v1:
time: 305 us
  waiting for transfers between devices  127 us (42%)
  matrix products  64.6 us (21%)
  blocking collectives  59.8 us (20%)
  starting transfers between devices  29.3 us (10%)
  between operations  14.2 us (5%)
  other arithmetic  5.62 us (2%)
  local copies, waits for them, and re-layouts  4.14 us (1%)
    ppermute x4, waiting for transfers between devices, from_behind(): lax.ppermute(value, axis, [(i, (i + by) % count) for i in range(count)])  95.3 us
    all_to_all x1, blocking collectives, shards(): lax.all_to_all(outgoing.reshape(experts, capacity, width), 'expert', spli...  59.8 us
    all_to_all x4, waiting for transfers between devices, shards(): lax.all_to_all(slot_grad.reshape(experts, capacity, step), 'expert', spli...  31.8 us
    all_to_all x4, starting transfers between devices, shards(): lax.all_to_all(slot_grad.reshape(experts, capacity, step), 'expert', spli...  18.5 us
    dot_general x4, matrix products, shards(): lax.dot_general(grad_gate_pre, gate_w[cols], along_hidden, preferred_elem...  16.5 us
    dot_general x1, matrix products, shards(): lax.dot_general(received, both_grads, along_slots, preferred_element_type...  15.6 us
    dot_general x4, matrix products, shards(): lax.dot_general(grad_up_pre, up_w[cols], along_hidden, preferred_element_...  14.3 us
    ppermute x4, starting transfers between devices, from_behind(): lax.ppermute(value, axis, [(i, (i + by) % count) for i in range(count)])  10.7 us
  transfers between devices with their start and end apart: 9, of which 8 were waited for; matrix products, arithmetic and copies ran while one was open for 13% of the time, Pallas kernels for 0%

profile of v1, /device:TPU:1, one launch (start us, length us, event | category | flops | bytes accessed | tf_op | source)
XLA Modules:
  0.0 304.7 jit_solution(5019949024572641585)
XLA Ops:
  7.2 0.0 copy-start
  7.2 0.0 reduce-scatter.2.cloned.1.call-start
  7.2 0.8 convert_reduce_fusion
  8.0 0.6 reduce-window.6
  8.6 0.2 slice_reduce_fusion
  8.9 0.1 bitcast_subtract_fusion
  8.9 0.7 select_reduce_fusion
  9.7 0.7 fusion.48
  10.3 0.2 fusion.47
  10.6 0.0 copy-start.2
  10.6 1.4 convolution_convert_fusion.1
  11.9 0.0 slice-start
  12.0 59.8 %all_to_all.25 = bf16[8,80,3584]{2,1,0:T(8,128)(2,1)S(1)} all-to-all(bf16[8,80,3584]{2,1,0:T(8,128)(2,1)S(1)} %bitcast.99), channel_id=1, replica_groups=mesh['section'=2,'dp'=8,'expert'=8] {'expert'}, dimensions={0} | all-to-all | bytes 9175040 | tf_op jit(solution)/shard_map/all_to_all | solution.py:42
  71.7 6.4 %fusion.8 = (bf16[640,1024]{1,0:T(8,128)(2,1)}, f32[640,1024]{1,0:T(8,128)S(1)}) fusion(bf16[1,1,1,640,1024]{4,3,2,1,0:T(8,128)(2,1)S(1)} %copy-done.3, bf16[640,3584]{1,0:T(8,128)(2,1)S(1)} %bitcast.100, bf16[1,1,3584,1024]{3,2,1,0:T(8,128)(2,1)S(1)} %copy-done.2), kind=kOutput, calls=%fused_computation.12 | convolution fusion | flops 4702208000 | bytes 17170432 | tf_op jit(solution)/shard_map/dot_general | solution.py:53
  78.2 5.5 %fusion.6 = bf16[640,1024]{1,0:T(8,128)(2,1)S(1)} fusion(f32[640,1024]{1,0:T(8,128)S(1)} %get-tuple-element.6, bf16[640,3584]{1,0:T(8,128)(2,1)S(1)} %bitcast.101, bf16[1,1,3584,1024]{3,2,1,0:T(8,128)(2,1)S(1)} %bitcast.112, bf16[1,1,1,640,1024]{4,3,2,1,0:T(8,128)(2,1)S(1)} %copy-done.3), kind=kOutput, calls=%fused_computation.10 | convolution fusion | flops 4704829440 | bytes 17170432 | tf_op jit(solution)/shard_map/dot_general | solution.py:54
  83.7 1.0 copy-done.4
  84.7 15.6 %convolution_convert_fusion = bf16[3584,2048]{1,0:T(8,128)(2,1)} fusion(bf16[640,3584]{1,0:T(8,128)(2,1)S(1)} %bitcast.102, bf16[640,1024]{1,0:T(8,128)(2,1)} %get-tuple-element.5, bf16[640,1024]{1,0:T(8,128)(2,1)S(1)} %fusion.6), kind=kOutput, calls=%fused_computation | convolution fusion | flops 9407823872 | bytes 21889024 | tf_op jit(solution)/shard_map/dot_general | solution.py:61
  100.3 0.0 reduce-scatter.2.cloned.1.call-update
  100.3 3.5 %fusion.24 = f32[640,896]{1,0:T(8,128)S(1)} fusion(bf16[640,1024]{1,0:T(8,128)(2,1)} %get-tuple-element.5, bf16[1,1,3584,1024]{3,2,1,0:T(8,128)(2,1)} %param.9), kind=kOutput, calls=%fused_computation.34 | convolution fusion | flops 1174405120 | bytes 5439488 | tf_op jit(solution)/shard_map/dot_general | solution.py:80
  103.9 4.1 %add_convert_fusion.3 = bf16[640,896]{1,0:T(8,128)(2,1)} fusion(f32[640,896]{1,0:T(8,128)S(1)} %fusion.24, bf16[640,1024]{1,0:T(8,128)(2,1)S(1)} %copy-done.5, bf16[1,1,3584,1024]{3,2,1,0:T(8,128)(2,1)} %param.8), kind=kOutput, calls=%fused_computation.20 | convolution fusion | flops 1175552000 | bytes 6586368 | tf_op jit(solution)/shard_map/dot_general | solution.py:79
  108.0 4.4 %all-to-all-start.1 = ((bf16[8,80,896]{2,1,0:T(8,128)(2,1)}), bf16[8,80,896]{2,1,0:T(8,128)(2,1)S(1)}, u32[]{:S(2)}, u32[]{:S(2)}) async-start(bf16[8,80,896]{2,1,0:T(8,128)(2,1)} %bitcast.16), calls=%async_computation.1 | async-start | bytes 2293760 | tf_op jit(solution)/shard_map/all_to_all | solution.py:82
  112.4 3.5 %fusion.20 = f32[640,896]{1,0:T(8,128)S(1)} fusion(bf16[640,1024]{1,0:T(8,128)(2,1)} %get-tuple-element.5, bf16[1,1,3584,1024]{3,2,1,0:T(8,128)(2,1)} %param.9), kind=kOutput, calls=%fused_computation.30 | convolution fusion | flops 1174405120 | bytes 5439488 | tf_op jit(solution)/shard_map/dot_general | solution.py:80
  116.0 4.2 %add_convert_fusion.2 = bf16[640,896]{1,0:T(8,128)(2,1)} fusion(f32[640,896]{1,0:T(8,128)S(1)} %fusion.20, bf16[640,1024]{1,0:T(8,128)(2,1)S(1)} %copy-done.6, bf16[1,1,3584,1024]{3,2,1,0:T(8,128)(2,1)} %param.8), kind=kOutput, calls=%fused_computation.19 | convolution fusion | flops 1175552000 | bytes 6586368 | tf_op jit(solution)/shard_map/dot_general | solution.py:79
  120.1 8.5 %all-to-all-done.1 = bf16[8,80,896]{2,1,0:T(8,128)(2,1)S(1)} async-done(((bf16[8,80,896]{2,1,0:T(8,128)(2,1)}), bf16[8,80,896]{2,1,0:T(8,128)(2,1)S(1)}, u32[]{:S(2)}, u32[]{:S(2)}) %all-to-all-start.1) | async-done | bytes 1146912 | tf_op jit(solution)/shard_map/all_to_all | solution.py:82
  128.7 4.2 %all-to-all-start.2 = ((bf16[8,80,896]{2,1,0:T(8,128)(2,1)}), bf16[8,80,896]{2,1,0:T(8,128)(2,1)S(1)}, u32[]{:S(2)}, u32[]{:S(2)}) async-start(bf16[8,80,896]{2,1,0:T(8,128)(2,1)} %bitcast.107), calls=%async_computation.2 | async-start | bytes 2293760 | tf_op jit(solution)/shard_map/all_to_all | solution.py:82
  132.9 3.5 %fusion.16 = f32[640,896]{1,0:T(8,128)S(1)} fusion(bf16[640,1024]{1,0:T(8,128)(2,1)} %get-tuple-element.5, bf16[1,1,3584,1024]{3,2,1,0:T(8,128)(2,1)} %param.9), kind=kOutput, calls=%fused_computation.26 | convolution fusion | flops 1174405120 | bytes 5439488 | tf_op jit(solution)/shard_map/dot_general | solution.py:80
  136.5 4.1 %add_convert_fusion.1 = bf16[640,896]{1,0:T(8,128)(2,1)} fusion(f32[640,896]{1,0:T(8,128)S(1)} %fusion.16, bf16[640,1024]{1,0:T(8,128)(2,1)S(1)} %copy-done.7, bf16[1,1,3584,1024]{3,2,1,0:T(8,128)(2,1)} %param.8), kind=kOutput, calls=%fused_computation.18 | convolution fusion | flops 1175552000 | bytes 6586368 | tf_op jit(solution)/shard_map/dot_general | solution.py:79
  140.6 8.6 %all-to-all-done.2 = bf16[8,80,896]{2,1,0:T(8,128)(2,1)S(1)} async-done(((bf16[8,80,896]{2,1,0:T(8,128)(2,1)}), bf16[8,80,896]{2,1,0:T(8,128)(2,1)S(1)}, u32[]{:S(2)}, u32[]{:S(2)}) %all-to-all-start.2) | async-done | bytes 1146912 | tf_op jit(solution)/shard_map/all_to_all | solution.py:82
  149.2 4.9 %all-to-all-start.3 = ((bf16[8,80,896]{2,1,0:T(8,128)(2,1)}), bf16[8,80,896]{2,1,0:T(8,128)(2,1)}, u32[]{:S(2)}, u32[]{:S(2)}) async-start(bf16[8,80,896]{2,1,0:T(8,128)(2,1)} %bitcast.106), calls=%async_computation.3 | async-start | bytes 2293760 | tf_op jit(solution)/shard_map/all_to_all | solution.py:82
  154.1 3.6 %fusion.12 = f32[640,896]{1,0:T(8,128)S(1)} fusion(bf16[640,1024]{1,0:T(8,128)(2,1)} %get-tuple-element.5, bf16[1,1,3584,1024]{3,2,1,0:T(8,128)(2,1)} %param.9), kind=kOutput, calls=%fused_computation.22 | convolution fusion | flops 1174405120 | bytes 5439488 | tf_op jit(solution)/shard_map/dot_general | solution.py:80
  157.7 4.1 %add_convert_fusion = bf16[640,896]{1,0:T(8,128)(2,1)} fusion(f32[640,896]{1,0:T(8,128)S(1)} %fusion.12, bf16[640,1024]{1,0:T(8,128)(2,1)S(1)} %copy-done.8, bf16[1,1,3584,1024]{3,2,1,0:T(8,128)(2,1)} %param.8), kind=kOutput, calls=%fused_computation.17 | convolution fusion | flops 1175552000 | bytes 6586368 | tf_op jit(solution)/shard_map/dot_general | solution.py:79
  161.9 8.5 %all-to-all-done.3 = bf16[8,80,896]{2,1,0:T(8,128)(2,1)} async-done(((bf16[8,80,896]{2,1,0:T(8,128)(2,1)}), bf16[8,80,896]{2,1,0:T(8,128)(2,1)}, u32[]{:S(2)}, u32[]{:S(2)}) %all-to-all-start.3) | async-done | bytes 1146912 | tf_op jit(solution)/shard_map/all_to_all | solution.py:82
  170.4 5.0 %all-to-all-start.4 = ((bf16[8,80,896]{2,1,0:T(8,128)(2,1)}), bf16[8,80,896]{2,1,0:T(8,128)(2,1)}, u32[]{:S(2)}, u32[]{:S(2)}) async-start(bf16[8,80,896]{2,1,0:T(8,128)(2,1)} %bitcast.105), calls=%async_computation.4 | async-start | bytes 2293760 | tf_op jit(solution)/shard_map/all_to_all | solution.py:82
  175.4 0.6 convolution_convert_fusion.5
  176.0 3.9 %collective-permute-start = (bf16[256,896]{1,0:T(8,128)(2,1)S(1)}, bf16[256,896]{1,0:T(8,128)(2,1)}, u32[]{:S(2)}, u32[]{:S(2)}) collective-permute-start(bf16[256,896]{1,0:T(8,128)(2,1)S(1)} %convolution_convert_fusion.5), channel_id=1, source_target_pairs={{0,64},{64,0},{1,65},{65,1},{2,66},{66,2},{3,67},{67,3},{4,68},{68... | collective-permute-start | bytes 1376264 | tf_op jit(solution)/shard_map/ppermute | solution.py:9
  179.9 0.6 convolution_convert_fusion.4
  180.5 0.1 collective-permute-start.1
  180.6 1.9 convolution_convert_fusion.3
  182.5 3.0 collective-permute-start.2
  185.5 6.2 %all-to-all-done.4 = bf16[8,80,896]{2,1,0:T(8,128)(2,1)} async-done(((bf16[8,80,896]{2,1,0:T(8,128)(2,1)}), bf16[8,80,896]{2,1,0:T(8,128)(2,1)}, u32[]{:S(2)}, u32[]{:S(2)}) %all-to-all-start.4) | async-done | bytes 1146912 | tf_op jit(solution)/shard_map/all_to_all | solution.py:82
  191.7 1.9 convolution_convert_fusion.2
  193.5 3.7 %collective-permute-start.3 = (bf16[256,896]{1,0:T(8,128)(2,1)S(1)}, bf16[256,896]{1,0:T(8,128)(2,1)S(1)}, u32[]{:S(2)}, u32[]{:S(2)}) collective-permute-start(bf16[256,896]{1,0:T(8,128)(2,1)S(1)} %convolution_convert_fusion.2), channel_id=1, source_target_pairs={{0,64},{64,0},{1,65},{65,1},{2,66},{66,2},{3,67},{67,3},{4,68},{68... | collective-permute-start | bytes 1376264 | tf_op jit(solution)/shard_map/ppermute | solution.py:9
  197.2 65.9 %collective-permute-done = bf16[256,896]{1,0:T(8,128)(2,1)} collective-permute-done((bf16[256,896]{1,0:T(8,128)(2,1)S(1)}, bf16[256,896]{1,0:T(8,128)(2,1)}, u32[]{:S(2)}, u32[]{:S(2)}) %collective-permute-start) | collective-permute-done | bytes 458784 | tf_op jit(solution)/shard_map/ppermute | solution.py:9
  263.1 9.7 %collective-permute-done.1 = bf16[256,896]{1,0:T(8,128)(2,1)S(1)} collective-permute-done((bf16[256,896]{1,0:T(8,128)(2,1)S(1)}, bf16[256,896]{1,0:T(8,128)(2,1)S(1)}, u32[]{:S(2)}, u32[]{:S(2)}) %collective-permute-start.1) | collective-permute-done | bytes 458784 | tf_op jit(solution)/shard_map/ppermute | solution.py:9
  272.9 9.8 %collective-permute-done.2 = bf16[256,896]{1,0:T(8,128)(2,1)S(1)} collective-permute-done((bf16[256,896]{1,0:T(8,128)(2,1)S(1)}, bf16[256,896]{1,0:T(8,128)(2,1)S(1)}, u32[]{:S(2)}, u32[]{:S(2)}) %collective-permute-start.2) | collective-permute-done | bytes 458784 | tf_op jit(solution)/shard_map/ppermute | solution.py:9
  282.7 9.8 %collective-permute-done.3 = bf16[256,896]{1,0:T(8,128)(2,1)S(1)} collective-permute-done((bf16[256,896]{1,0:T(8,128)(2,1)S(1)}, bf16[256,896]{1,0:T(8,128)(2,1)S(1)}, u32[]{:S(2)}, u32[]{:S(2)}) %collective-permute-start.3) | collective-permute-done | bytes 458784 | tf_op jit(solution)/shard_map/ppermute | solution.py:9
  292.5 2.5 maximum_bitcast_fusion
  295.0 2.8 slice_bitcast_fusion
  (22 shorter events, 0.1 us)
Async XLA Ops:
  7.2 3.4 %copy-start = (bf16[1,256,3584]{2,1,0:T(8,128)(2,1)S(1)}, bf16[1,256,3584]{2,1,0:T(8,128)(2,1)}, u32[]{:S(2)}) copy-start(bf16[1,256,3584]{2,1,0:T(8,128)(2,1)} %param.5) | copy-start | bytes 5505028
  7.2 287.9 %reduce-scatter.2.cloned.1.call-start = ((), (), s32[]{:S(2)}) async-start(), calls=%async_computation.6 | async-start | bytes 16515072 | tf_op jit(solution)/shard_map/reduce_scatter | solution.py:60
  10.6 61.2 %copy-start.2 = (bf16[1,1,3584,1024]{3,2,1,0:T(8,128)(2,1)S(1)}, bf16[1,1,3584,1024]{3,2,1,0:T(8,128)(2,1)}, u32[]{:S(2)}) copy-start(bf16[1,1,3584,1024]{3,2,1,0:T(8,128)(2,1)} %param.8) | copy-start | bytes 22020100
  11.9 59.8 %copy-start.3 = (bf16[1,1,1,640,1024]{4,3,2,1,0:T(8,128)(2,1)S(1)}, bf16[1,1,1,640,1024]{4,3,2,1,0:T(8,128)(2,1)}, u32[]{:S(2)}) copy-start(bf16[1,1,1,640,1024]{4,3,2,1,0:T(8,128)(2,1)} %param.7) | copy-start | bytes 3932164
  11.9 66.2 %slice-start = ((s8[7340032]{0:T(1024)(128)(4,1)}), s8[4194304]{0:T(1024)(128)(4,1)S(1)}, s32[]{:S(2)}) async-start(s8[7340032]{0:T(1024)(128)(4,1)} %bitcast.111), calls=%async_computation.7 | async-start | bytes 8388608
  71.7 6.4 %slice-start.1 = ((s8[7340032]{0:T(1024)(128)(4,1)}), s8[3145728]{0:T(1024)(128)(4,1)S(1)}, s32[]{:S(2)}) async-start(s8[7340032]{0:T(1024)(128)(4,1)} %bitcast.111), calls=%async_computation.8 | async-start | bytes 6291456
  83.7 1.1 copy-start.4
  100.3 3.6 %copy-start.5 = (bf16[640,1024]{1,0:T(8,128)(2,1)S(1)}, bf16[640,1024]{1,0:T(8,128)(2,1)}, u32[]{:S(2)}) copy-start(bf16[640,1024]{1,0:T(8,128)(2,1)} %copy-done.4) | copy-start | bytes 3932164
  108.0 20.7 %all-to-all-start.1 = ((bf16[8,80,896]{2,1,0:T(8,128)(2,1)}), bf16[8,80,896]{2,1,0:T(8,128)(2,1)S(1)}, u32[]{:S(2)}, u32[]{:S(2)}) async-start(bf16[8,80,896]{2,1,0:T(8,128)(2,1)} %bitcast.16), calls=%async_computation.1 | async-start | bytes 2293760 | tf_op jit(solution)/shard_map/all_to_all | solution.py:82
  112.4 3.6 %copy-start.6 = (bf16[640,1024]{1,0:T(8,128)(2,1)S(1)}, bf16[640,1024]{1,0:T(8,128)(2,1)}, u32[]{:S(2)}) copy-start(bf16[640,1024]{1,0:T(8,128)(2,1)} %copy-done.4) | copy-start | bytes 3932164
  128.7 20.5 %all-to-all-start.2 = ((bf16[8,80,896]{2,1,0:T(8,128)(2,1)}), bf16[8,80,896]{2,1,0:T(8,128)(2,1)S(1)}, u32[]{:S(2)}, u32[]{:S(2)}) async-start(bf16[8,80,896]{2,1,0:T(8,128)(2,1)} %bitcast.107), calls=%async_computation.2 | async-start | bytes 2293760 | tf_op jit(solution)/shard_map/all_to_all | solution.py:82
  132.9 3.6 %copy-start.7 = (bf16[640,1024]{1,0:T(8,128)(2,1)S(1)}, bf16[640,1024]{1,0:T(8,128)(2,1)}, u32[]{:S(2)}) copy-start(bf16[640,1024]{1,0:T(8,128)(2,1)} %copy-done.4) | copy-start | bytes 3932164
  149.2 21.2 %all-to-all-start.3 = ((bf16[8,80,896]{2,1,0:T(8,128)(2,1)}), bf16[8,80,896]{2,1,0:T(8,128)(2,1)}, u32[]{:S(2)}, u32[]{:S(2)}) async-start(bf16[8,80,896]{2,1,0:T(8,128)(2,1)} %bitcast.106), calls=%async_computation.3 | async-start | bytes 2293760 | tf_op jit(solution)/shard_map/all_to_all | solution.py:82
  154.1 3.6 %copy-start.8 = (bf16[640,1024]{1,0:T(8,128)(2,1)S(1)}, bf16[640,1024]{1,0:T(8,128)(2,1)}, u32[]{:S(2)}) copy-start(bf16[640,1024]{1,0:T(8,128)(2,1)} %copy-done.4) | copy-start | bytes 3932164
  170.4 21.3 %all-to-all-start.4 = ((bf16[8,80,896]{2,1,0:T(8,128)(2,1)}), bf16[8,80,896]{2,1,0:T(8,128)(2,1)}, u32[]{:S(2)}, u32[]{:S(2)}) async-start(bf16[8,80,896]{2,1,0:T(8,128)(2,1)} %bitcast.105), calls=%async_computation.4 | async-start | bytes 2293760 | tf_op jit(solution)/shard_map/all_to_all | solution.py:82
  176.0 87.1 %collective-permute-start = (bf16[256,896]{1,0:T(8,128)(2,1)S(1)}, bf16[256,896]{1,0:T(8,128)(2,1)}, u32[]{:S(2)}, u32[]{:S(2)}) collective-permute-start(bf16[256,896]{1,0:T(8,128)(2,1)S(1)} %convolution_convert_fusion.5), channel_id=1, source_target_pairs={{0,64},{64,0},{1,65},{65,1},{2,66},{66,2},{3,67},{67,3},{4,68},{68... | collective-permute-start | bytes 1376264 | tf_op jit(solution)/shard_map/ppermute | solution.py:9
  180.5 92.4 %collective-permute-start.1 = (bf16[256,896]{1,0:T(8,128)(2,1)S(1)}, bf16[256,896]{1,0:T(8,128)(2,1)S(1)}, u32[]{:S(2)}, u32[]{:S(2)}) collective-permute-start(bf16[256,896]{1,0:T(8,128)(2,1)S(1)} %convolution_convert_fusion.4), channel_id=1, source_target_pairs={{0,64},{64,0},{1,65},{65,1},{2,66},{66,2},{3,67},{67,3},{4,68},{68... | collective-permute-start | bytes 1376264 | tf_op jit(solution)/shard_map/ppermute | solution.py:9
  182.5 100.2 %collective-permute-start.2 = (bf16[256,896]{1,0:T(8,128)(2,1)S(1)}, bf16[256,896]{1,0:T(8,128)(2,1)S(1)}, u32[]{:S(2)}, u32[]{:S(2)}) collective-permute-start(bf16[256,896]{1,0:T(8,128)(2,1)S(1)} %convolution_convert_fusion.3), channel_id=1, source_target_pairs={{0,64},{64,0},{1,65},{65,1},{2,66},{66,2},{3,67},{67,3},{4,68},{68... | collective-permute-start | bytes 1376264 | tf_op jit(solution)/shard_map/ppermute | solution.py:9
  193.5 99.0 %collective-permute-start.3 = (bf16[256,896]{1,0:T(8,128)(2,1)S(1)}, bf16[256,896]{1,0:T(8,128)(2,1)S(1)}, u32[]{:S(2)}, u32[]{:S(2)}) collective-permute-start(bf16[256,896]{1,0:T(8,128)(2,1)S(1)} %convolution_convert_fusion.2), channel_id=1, source_target_pairs={{0,64},{64,0},{1,65},{65,1},{2,66},{66,2},{3,67},{67,3},{4,68},{68... | collective-permute-start | bytes 1376264 | tf_op jit(solution)/shard_map/ppermute | solution.py:9
  292.5 5.3 %copy-start.1 = (bf16[1,256,3584]{2,1,0:T(8,128)(2,1)S(1)}, bf16[1,256,3584]{2,1,0:T(8,128)(2,1)}, u32[]{:S(2)}) copy-start(bf16[1,256,3584]{2,1,0:T(8,128)(2,1)} %param.5) | copy-start | bytes 5505028
Sparse Core Ops, SparseCore 0:
  100.5 152.7 reduce-scatter.1

commit v2 on v1

--- a/solution.py
+++ b/solution.py
@@ -7,6 +7,23 @@
 def from_behind(value, axis, by):
     count = lax.axis_size(axis)
     return lax.ppermute(value, axis, [(i, (i + by) % count) for i in range(count)])
+
+
+def across_sections(value, way):
+    sections = lax.axis_size("section")
+    groups = lax.axis_size("dp")
+    lows = 2
+    rows = groups // lows
+    ring = sections * lows
+
+    def place(z, x):
+        return (z // lows) * groups + (z % lows) * rows + x
+
+    perm = [
+        (place(z, x), place((z + way) % ring, x)) for z in range(ring) for x in range(rows)
+    ]
+    hop = lax.ppermute(value, ("section", "dp"), perm)
+    return lax.ppermute(hop, ("section", "dp"), perm)
 
 
 def slot_numbers(route_rows, experts, capacity):
@@ -89,7 +106,7 @@
         token_grad = jnp.dot(gather_back, returned, preferred_element_type=jnp.float32).astype(
             jnp.bfloat16
         )
-        passed.append(from_behind(token_grad, "section", -1))
+        passed.append(across_sections(token_grad, 1 if piece % 2 == 0 else -1))
     passed_grad = jnp.concatenate(passed, axis=1)[None]
     return (passed_grad, grad_gate, grad_up)
 

time: 305 us -> 303 us (level)
    ppermute x4 -> x8, waiting for transfers between devices: 95.3 us -> 92.8 us  [the longest x4 74.6 us: across_sections(): hop = lax.ppermute(value, ('section', 'dp'), perm)]
    ppermute x4 -> x8, starting transfers between devices: 10.7 us -> 11.2 us  [the longest x4 8.24 us: across_sections(): hop = lax.ppermute(value, ('section', 'dp'), perm)]
  transfers between devices with their start and end apart: 9 -> 13, of which waited for: 8 -> 8; matrix products, arithmetic and copies ran while one was open for 13% -> 13% of each run, Pallas kernels for 0% -> 0%
where the time goes in v2:
time: 303 us; the launch traced here: 302 us
  waiting for transfers between devices  124 us (41%)
  matrix products  65.4 us (22%)
  blocking collectives  59.8 us (20%)
  starting transfers between devices  29.7 us (10%)
  between operations  14.2 us (5%)
  other arithmetic  4.47 us (1%)
  local copies, waits for them, and re-layouts  4.15 us (1%)
    ppermute x4, waiting for transfers between devices, across_sections(): hop = lax.ppermute(value, ('section', 'dp'), perm)  74.6 us
    all_to_all x1, blocking collectives, shards(): lax.all_to_all(outgoing.reshape(experts, capacity, width), 'expert', spli...  59.8 us
    all_to_all x4, waiting for transfers between devices, shards(): lax.all_to_all(slot_grad.reshape(experts, capacity, step), 'expert', spli...  31.5 us
    all_to_all x4, starting transfers between devices, shards(): lax.all_to_all(slot_grad.reshape(experts, capacity, step), 'expert', spli...  18.5 us
    ppermute x4, waiting for transfers between devices, across_sections(): return lax.ppermute(hop, ('section', 'dp'), perm)  18.2 us
    dot_general x4, matrix products, shards(): lax.dot_general(grad_gate_pre, gate_w[cols], along_hidden, preferred_elem...  16.6 us
    dot_general x1, matrix products, shards(): lax.dot_general(received, both_grads, along_slots, preferred_element_type...  15.6 us
    dot_general x4, matrix products, shards(): lax.dot_general(grad_up_pre, up_w[cols], along_hidden, preferred_element_...  14.3 us
  transfers between devices with their start and end apart: 13, of which 8 were waited for; matrix products, arithmetic and copies ran while one was open for 13% of the time, Pallas kernels for 0%

profile of v2, /device:TPU:1, one launch (start us, length us, event | category | flops | bytes accessed | tf_op | source)
XLA Modules:
  0.0 302.0 jit_solution(9884738185613640903)
XLA Ops:
  7.2 0.0 reduce-scatter.2.cloned.1.call-start
  7.2 0.8 convert_reduce_fusion
  8.0 0.6 reduce-window.6
  8.6 0.2 slice_reduce_fusion
  8.9 0.1 bitcast_subtract_fusion
  8.9 0.7 select_reduce_fusion
  9.7 0.7 fusion.48
  10.3 0.2 fusion.47
  10.6 1.4 convolution_convert_fusion.1
  12.0 59.8 %all_to_all.25 = bf16[8,80,3584]{2,1,0:T(8,128)(2,1)S(1)} all-to-all(bf16[8,80,3584]{2,1,0:T(8,128)(2,1)S(1)} %bitcast.99), channel_id=1, replica_groups=mesh['section'=2,'dp'=8,'expert'=8] {'expert'}, dimensions={0} | all-to-all | bytes 9175040 | tf_op jit(solution)/shard_map/all_to_all | solution.py:59
  71.7 6.4 %fusion.8 = (bf16[640,1024]{1,0:T(8,128)(2,1)}, f32[640,1024]{1,0:T(8,128)S(1)}) fusion(bf16[1,1,1,640,1024]{4,3,2,1,0:T(8,128)(2,1)S(1)} %copy-done.3, bf16[640,3584]{1,0:T(8,128)(2,1)S(1)} %bitcast.100, bf16[1,1,3584,1024]{3,2,1,0:T(8,128)(2,1)S(1)} %copy-done.2), kind=kOutput, calls=%fused_computation.12 | convolution fusion | flops 4702208000 | bytes 17170432 | tf_op jit(solution)/shard_map/dot_general | solution.py:70
  78.2 5.5 %fusion.6 = bf16[640,1024]{1,0:T(8,128)(2,1)S(1)} fusion(f32[640,1024]{1,0:T(8,128)S(1)} %get-tuple-element.6, bf16[640,3584]{1,0:T(8,128)(2,1)S(1)} %bitcast.101, bf16[1,1,3584,1024]{3,2,1,0:T(8,128)(2,1)S(1)} %bitcast.112, bf16[1,1,1,640,1024]{4,3,2,1,0:T(8,128)(2,1)S(1)} %copy-done.3), kind=kOutput, calls=%fused_computation.10 | convolution fusion | flops 4704829440 | bytes 17170432 | tf_op jit(solution)/shard_map/dot_general | solution.py:71
  83.7 1.1 copy-done.4
  84.7 15.6 %convolution_convert_fusion = bf16[3584,2048]{1,0:T(8,128)(2,1)} fusion(bf16[640,3584]{1,0:T(8,128)(2,1)S(1)} %bitcast.102, bf16[640,1024]{1,0:T(8,128)(2,1)} %get-tuple-element.5, bf16[640,1024]{1,0:T(8,128)(2,1)S(1)} %fusion.6), kind=kOutput, calls=%fused_computation | convolution fusion | flops 9407823872 | bytes 21889024 | tf_op jit(solution)/shard_map/dot_general | solution.py:78
  100.3 3.5 %fusion.12 = f32[640,896]{1,0:T(8,128)S(1)} fusion(bf16[640,1024]{1,0:T(8,128)(2,1)} %get-tuple-element.5, bf16[1,1,3584,1024]{3,2,1,0:T(8,128)(2,1)} %param.9), kind=kOutput, calls=%fused_computation.22 | convolution fusion | flops 1174405120 | bytes 5439488 | tf_op jit(solution)/shard_map/dot_general | solution.py:97
  103.9 4.1 %add_convert_fusion = bf16[640,896]{1,0:T(8,128)(2,1)} fusion(f32[640,896]{1,0:T(8,128)S(1)} %fusion.12, bf16[640,1024]{1,0:T(8,128)(2,1)S(1)} %copy-done.5, bf16[1,1,3584,1024]{3,2,1,0:T(8,128)(2,1)} %param.8), kind=kOutput, calls=%fused_computation.17 | convolution fusion | flops 1175552000 | bytes 6586368 | tf_op jit(solution)/shard_map/dot_general | solution.py:96
  108.0 4.4 %all-to-all-start.4 = ((bf16[8,80,896]{2,1,0:T(8,128)(2,1)}), bf16[8,80,896]{2,1,0:T(8,128)(2,1)S(1)}, u32[]{:S(2)}, u32[]{:S(2)}) async-start(bf16[8,80,896]{2,1,0:T(8,128)(2,1)} %bitcast.28), calls=%async_computation.4 | async-start | bytes 2293760 | tf_op jit(solution)/shard_map/all_to_all | solution.py:99
  112.4 3.5 %fusion.16 = f32[640,896]{1,0:T(8,128)S(1)} fusion(bf16[640,1024]{1,0:T(8,128)(2,1)} %get-tuple-element.5, bf16[1,1,3584,1024]{3,2,1,0:T(8,128)(2,1)} %param.9), kind=kOutput, calls=%fused_computation.26 | convolution fusion | flops 1174405120 | bytes 5439488 | tf_op jit(solution)/shard_map/dot_general | solution.py:97
  116.0 4.2 %add_convert_fusion.1 = bf16[640,896]{1,0:T(8,128)(2,1)} fusion(f32[640,896]{1,0:T(8,128)S(1)} %fusion.16, bf16[640,1024]{1,0:T(8,128)(2,1)S(1)} %copy-done.6, bf16[1,1,3584,1024]{3,2,1,0:T(8,128)(2,1)} %param.8), kind=kOutput, calls=%fused_computation.18 | convolution fusion | flops 1175552000 | bytes 6586368 | tf_op jit(solution)/shard_map/dot_general | solution.py:96
  120.1 8.6 %all-to-all-done.4 = bf16[8,80,896]{2,1,0:T(8,128)(2,1)S(1)} async-done(((bf16[8,80,896]{2,1,0:T(8,128)(2,1)}), bf16[8,80,896]{2,1,0:T(8,128)(2,1)S(1)}, u32[]{:S(2)}, u32[]{:S(2)}) %all-to-all-start.4) | async-done | bytes 1146912 | tf_op jit(solution)/shard_map/all_to_all | solution.py:99
  128.7 4.2 %all-to-all-start.3 = ((bf16[8,80,896]{2,1,0:T(8,128)(2,1)}), bf16[8,80,896]{2,1,0:T(8,128)(2,1)S(1)}, u32[]{:S(2)}, u32[]{:S(2)}) async-start(bf16[8,80,896]{2,1,0:T(8,128)(2,1)} %bitcast.107), calls=%async_computation.3 | async-start | bytes 2293760 | tf_op jit(solution)/shard_map/all_to_all | solution.py:99
  132.9 3.5 %fusion.20 = f32[640,896]{1,0:T(8,128)S(1)} fusion(bf16[640,1024]{1,0:T(8,128)(2,1)} %get-tuple-element.5, bf16[1,1,3584,1024]{3,2,1,0:T(8,128)(2,1)} %param.9), kind=kOutput, calls=%fused_computation.30 | convolution fusion | flops 1174405120 | bytes 5439488 | tf_op jit(solution)/shard_map/dot_general | solution.py:97
  136.5 4.2 %add_convert_fusion.2 = bf16[640,896]{1,0:T(8,128)(2,1)} fusion(f32[640,896]{1,0:T(8,128)S(1)} %fusion.20, bf16[640,1024]{1,0:T(8,128)(2,1)S(1)} %copy-done.7, bf16[1,1,3584,1024]{3,2,1,0:T(8,128)(2,1)} %param.8), kind=kOutput, calls=%fused_computation.19 | convolution fusion | flops 1175552000 | bytes 6586368 | tf_op jit(solution)/shard_map/dot_general | solution.py:96
  140.6 8.6 %all-to-all-done.3 = bf16[8,80,896]{2,1,0:T(8,128)(2,1)S(1)} async-done(((bf16[8,80,896]{2,1,0:T(8,128)(2,1)}), bf16[8,80,896]{2,1,0:T(8,128)(2,1)S(1)}, u32[]{:S(2)}, u32[]{:S(2)}) %all-to-all-start.3) | async-done | bytes 1146912 | tf_op jit(solution)/shard_map/all_to_all | solution.py:99
  149.2 4.9 %all-to-all-start.2 = ((bf16[8,80,896]{2,1,0:T(8,128)(2,1)}), bf16[8,80,896]{2,1,0:T(8,128)(2,1)}, u32[]{:S(2)}, u32[]{:S(2)}) async-start(bf16[8,80,896]{2,1,0:T(8,128)(2,1)} %bitcast.106), calls=%async_computation.2 | async-start | bytes 2293760 | tf_op jit(solution)/shard_map/all_to_all | solution.py:99
  154.1 3.6 %fusion.24 = f32[640,896]{1,0:T(8,128)S(1)} fusion(bf16[640,1024]{1,0:T(8,128)(2,1)} %get-tuple-element.5, bf16[1,1,3584,1024]{3,2,1,0:T(8,128)(2,1)} %param.9), kind=kOutput, calls=%fused_computation.34 | convolution fusion | flops 1174405120 | bytes 5439488 | tf_op jit(solution)/shard_map/dot_general | solution.py:97
  157.7 4.1 %add_convert_fusion.3 = bf16[640,896]{1,0:T(8,128)(2,1)} fusion(f32[640,896]{1,0:T(8,128)S(1)} %fusion.24, bf16[640,1024]{1,0:T(8,128)(2,1)S(1)} %copy-done.8, bf16[1,1,3584,1024]{3,2,1,0:T(8,128)(2,1)} %param.8), kind=kOutput, calls=%fused_computation.20 | convolution fusion | flops 1175552000 | bytes 6586368 | tf_op jit(solution)/shard_map/dot_general | solution.py:96
  161.9 8.5 %all-to-all-done.2 = bf16[8,80,896]{2,1,0:T(8,128)(2,1)} async-done(((bf16[8,80,896]{2,1,0:T(8,128)(2,1)}), bf16[8,80,896]{2,1,0:T(8,128)(2,1)}, u32[]{:S(2)}, u32[]{:S(2)}) %all-to-all-start.2) | async-done | bytes 1146912 | tf_op jit(solution)/shard_map/all_to_all | solution.py:99
  170.4 5.0 %all-to-all-start.1 = ((bf16[8,80,896]{2,1,0:T(8,128)(2,1)}), bf16[8,80,896]{2,1,0:T(8,128)(2,1)}, u32[]{:S(2)}, u32[]{:S(2)}) async-start(bf16[8,80,896]{2,1,0:T(8,128)(2,1)} %bitcast.105), calls=%async_computation.1 | async-start | bytes 2293760 | tf_op jit(solution)/shard_map/all_to_all | solution.py:99
  175.4 1.4 convolution_convert_fusion.2
  176.7 3.7 %collective-permute-start.6 = (bf16[256,896]{1,0:T(8,128)(2,1)}, bf16[256,896]{1,0:T(8,128)(2,1)S(1)}, u32[]{:S(2)}, u32[]{:S(2)}) collective-permute-start(bf16[256,896]{1,0:T(8,128)(2,1)} %convolution_convert_fusion.2), channel_id=1, source_target_pairs={{0,96},{8,104},{16,112},{24,120},{32,0},{40,8},{48,16},{56,24},{64... | collective-permute-start | bytes 1376264 | tf_op jit(solution)/shard_map/ppermute | solution.py:25
  180.5 0.6 convolution_convert_fusion.3
  181.1 0.1 collective-permute-start.4
  181.2 1.9 convolution_convert_fusion.4
  183.0 2.7 collective-permute-start.2
  185.8 5.9 %all-to-all-done.1 = bf16[8,80,896]{2,1,0:T(8,128)(2,1)} async-done(((bf16[8,80,896]{2,1,0:T(8,128)(2,1)}), bf16[8,80,896]{2,1,0:T(8,128)(2,1)}, u32[]{:S(2)}, u32[]{:S(2)}) %all-to-all-start.1) | async-done | bytes 1146912 | tf_op jit(solution)/shard_map/all_to_all | solution.py:99
  191.6 1.9 convolution_convert_fusion.5
  193.5 1.7 collective-permute-start
  195.2 66.2 %collective-permute-done.6 = bf16[256,896]{1,0:T(8,128)(2,1)S(1)} collective-permute-done((bf16[256,896]{1,0:T(8,128)(2,1)}, bf16[256,896]{1,0:T(8,128)(2,1)S(1)}, u32[]{:S(2)}, u32[]{:S(2)}) %collective-permute-start.6) | collective-permute-done | bytes 458784 | tf_op jit(solution)/shard_map/ppermute | solution.py:25
  261.4 0.7 collective-permute-start.7
  262.2 0.7 collective-permute-start.5
  262.9 8.4 %collective-permute-done.2 = bf16[256,896]{1,0:T(8,128)(2,1)S(1)} collective-permute-done((bf16[256,896]{1,0:T(8,128)(2,1)S(1)}, bf16[256,896]{1,0:T(8,128)(2,1)S(1)}, u32[]{:S(2)}, u32[]{:S(2)}) %collective-permute-start.2) | collective-permute-done | bytes 458784 | tf_op jit(solution)/shard_map/ppermute | solution.py:25
  271.3 0.6 collective-permute-start.3
  271.9 0.8 collective-permute-start.1
  272.7 8.4 %collective-permute-done.7 = bf16[256,896]{1,0:T(8,128)(2,1)S(1)} collective-permute-done((bf16[256,896]{1,0:T(8,128)(2,1)S(1)}, bf16[256,896]{1,0:T(8,128)(2,1)S(1)}, u32[]{:S(2)}, u32[]{:S(2)}) %collective-permute-start.7) | collective-permute-done | bytes 458784 | tf_op jit(solution)/shard_map/ppermute | solution.py:26
  281.1 9.8 %collective-permute-done.3 = bf16[256,896]{1,0:T(8,128)(2,1)S(1)} collective-permute-done((bf16[256,896]{1,0:T(8,128)(2,1)S(1)}, bf16[256,896]{1,0:T(8,128)(2,1)S(1)}, u32[]{:S(2)}, u32[]{:S(2)}) %collective-permute-start.3) | collective-permute-done | bytes 458784 | tf_op jit(solution)/shard_map/ppermute | solution.py:26
  290.9 1.4 maximum_bitcast_fusion
  292.3 2.8 slice_bitcast_fusion
  (30 shorter events, 0.1 us)
Async XLA Ops:
  7.2 3.4 %copy-start = (bf16[1,256,3584]{2,1,0:T(8,128)(2,1)S(1)}, bf16[1,256,3584]{2,1,0:T(8,128)(2,1)}, u32[]{:S(2)}) copy-start(bf16[1,256,3584]{2,1,0:T(8,128)(2,1)} %param.5) | copy-start | bytes 5505028
  7.2 285.1 %reduce-scatter.2.cloned.1.call-start = ((), (), s32[]{:S(2)}) async-start(), calls=%async_computation.6 | async-start | bytes 16515072 | tf_op jit(solution)/shard_map/reduce_scatter | solution.py:77
  10.6 61.2 %copy-start.2 = (bf16[1,1,3584,1024]{3,2,1,0:T(8,128)(2,1)S(1)}, bf16[1,1,3584,1024]{3,2,1,0:T(8,128)(2,1)}, u32[]{:S(2)}) copy-start(bf16[1,1,3584,1024]{3,2,1,0:T(8,128)(2,1)} %param.8) | copy-start | bytes 22020100
  11.9 59.8 %copy-start.3 = (bf16[1,1,1,640,1024]{4,3,2,1,0:T(8,128)(2,1)S(1)}, bf16[1,1,1,640,1024]{4,3,2,1,0:T(8,128)(2,1)}, u32[]{:S(2)}) copy-start(bf16[1,1,1,640,1024]{4,3,2,1,0:T(8,128)(2,1)} %param.7) | copy-start | bytes 3932164
  11.9 66.2 %slice-start = ((s8[7340032]{0:T(1024)(128)(4,1)}), s8[4194304]{0:T(1024)(128)(4,1)S(1)}, s32[]{:S(2)}) async-start(s8[7340032]{0:T(1024)(128)(4,1)} %bitcast.111), calls=%async_computation.7 | async-start | bytes 8388608
  71.7 6.4 %slice-start.1 = ((s8[7340032]{0:T(1024)(128)(4,1)}), s8[3145728]{0:T(1024)(128)(4,1)S(1)}, s32[]{:S(2)}) async-start(s8[7340032]{0:T(1024)(128)(4,1)} %bitcast.111), calls=%async_computation.8 | async-start | bytes 6291456
  83.7 1.1 copy-start.4
  100.3 3.6 %copy-start.5 = (bf16[640,1024]{1,0:T(8,128)(2,1)S(1)}, bf16[640,1024]{1,0:T(8,128)(2,1)}, u32[]{:S(2)}) copy-start(bf16[640,1024]{1,0:T(8,128)(2,1)} %copy-done.4) | copy-start | bytes 3932164
  108.0 20.7 %all-to-all-start.4 = ((bf16[8,80,896]{2,1,0:T(8,128)(2,1)}), bf16[8,80,896]{2,1,0:T(8,128)(2,1)S(1)}, u32[]{:S(2)}, u32[]{:S(2)}) async-start(bf16[8,80,896]{2,1,0:T(8,128)(2,1)} %bitcast.28), calls=%async_computation.4 | async-start | bytes 2293760 | tf_op jit(solution)/shard_map/all_to_all | solution.py:99
  112.4 3.6 %copy-start.6 = (bf16[640,1024]{1,0:T(8,128)(2,1)S(1)}, bf16[640,1024]{1,0:T(8,128)(2,1)}, u32[]{:S(2)}) copy-start(bf16[640,1024]{1,0:T(8,128)(2,1)} %copy-done.4) | copy-start | bytes 3932164
  128.7 20.5 %all-to-all-start.3 = ((bf16[8,80,896]{2,1,0:T(8,128)(2,1)}), bf16[8,80,896]{2,1,0:T(8,128)(2,1)S(1)}, u32[]{:S(2)}, u32[]{:S(2)}) async-start(bf16[8,80,896]{2,1,0:T(8,128)(2,1)} %bitcast.107), calls=%async_computation.3 | async-start | bytes 2293760 | tf_op jit(solution)/shard_map/all_to_all | solution.py:99
  132.9 3.6 %copy-start.7 = (bf16[640,1024]{1,0:T(8,128)(2,1)S(1)}, bf16[640,1024]{1,0:T(8,128)(2,1)}, u32[]{:S(2)}) copy-start(bf16[640,1024]{1,0:T(8,128)(2,1)} %copy-done.4) | copy-start | bytes 3932164
  149.2 21.2 %all-to-all-start.2 = ((bf16[8,80,896]{2,1,0:T(8,128)(2,1)}), bf16[8,80,896]{2,1,0:T(8,128)(2,1)}, u32[]{:S(2)}, u32[]{:S(2)}) async-start(bf16[8,80,896]{2,1,0:T(8,128)(2,1)} %bitcast.106), calls=%async_computation.2 | async-start | bytes 2293760 | tf_op jit(solution)/shard_map/all_to_all | solution.py:99
  154.1 3.6 %copy-start.8 = (bf16[640,1024]{1,0:T(8,128)(2,1)S(1)}, bf16[640,1024]{1,0:T(8,128)(2,1)}, u32[]{:S(2)}) copy-start(bf16[640,1024]{1,0:T(8,128)(2,1)} %copy-done.4) | copy-start | bytes 3932164
  170.4 21.3 %all-to-all-start.1 = ((bf16[8,80,896]{2,1,0:T(8,128)(2,1)}), bf16[8,80,896]{2,1,0:T(8,128)(2,1)}, u32[]{:S(2)}, u32[]{:S(2)}) async-start(bf16[8,80,896]{2,1,0:T(8,128)(2,1)} %bitcast.105), calls=%async_computation.1 | async-start | bytes 2293760 | tf_op jit(solution)/shard_map/all_to_all | solution.py:99
  176.7 84.7 %collective-permute-start.6 = (bf16[256,896]{1,0:T(8,128)(2,1)}, bf16[256,896]{1,0:T(8,128)(2,1)S(1)}, u32[]{:S(2)}, u32[]{:S(2)}) collective-permute-start(bf16[256,896]{1,0:T(8,128)(2,1)} %convolution_convert_fusion.2), channel_id=1, source_target_pairs={{0,96},{8,104},{16,112},{24,120},{32,0},{40,8},{48,16},{56,24},{64... | collective-permute-start | bytes 1376264 | tf_op jit(solution)/shard_map/ppermute | solution.py:25
  181.1 81.1 %collective-permute-start.4 = (bf16[256,896]{1,0:T(8,128)(2,1)S(1)}, bf16[256,896]{1,0:T(8,128)(2,1)S(1)}, u32[]{:S(2)}, u32[]{:S(2)}) collective-permute-start(bf16[256,896]{1,0:T(8,128)(2,1)S(1)} %convolution_convert_fusion.3), channel_id=1, source_target_pairs={{0,32},{8,40},{16,48},{24,56},{32,64},{40,72},{48,80},{56,88},{64,... | collective-permute-start | bytes 1376264 | tf_op jit(solution)/shard_map/ppermute | solution.py:25
  183.0 88.2 %collective-permute-start.2 = (bf16[256,896]{1,0:T(8,128)(2,1)S(1)}, bf16[256,896]{1,0:T(8,128)(2,1)S(1)}, u32[]{:S(2)}, u32[]{:S(2)}) collective-permute-start(bf16[256,896]{1,0:T(8,128)(2,1)S(1)} %convolution_convert_fusion.4), channel_id=1, source_target_pairs={{0,96},{8,104},{16,112},{24,120},{32,0},{40,8},{48,16},{56,24},{64... | collective-permute-start | bytes 1376264 | tf_op jit(solution)/shard_map/ppermute | solution.py:25
  193.5 78.4 %collective-permute-start = (bf16[256,896]{1,0:T(8,128)(2,1)S(1)}, bf16[256,896]{1,0:T(8,128)(2,1)S(1)}, u32[]{:S(2)}, u32[]{:S(2)}) collective-permute-start(bf16[256,896]{1,0:T(8,128)(2,1)S(1)} %convolution_convert_fusion.5), channel_id=1, source_target_pairs={{0,32},{8,40},{16,48},{24,56},{32,64},{40,72},{48,80},{56,88},{64,... | collective-permute-start | bytes 1376264 | tf_op jit(solution)/shard_map/ppermute | solution.py:25
  261.4 19.7 %collective-permute-start.7 = (bf16[256,896]{1,0:T(8,128)(2,1)S(1)}, bf16[256,896]{1,0:T(8,128)(2,1)S(1)}, u32[]{:S(2)}, u32[]{:S(2)}) collective-permute-start(bf16[256,896]{1,0:T(8,128)(2,1)S(1)} %collective-permute-done.6), channel_id=1, source_target_pairs={{0,96},{8,104},{16,112},{24,120},{32,0},{40,8},{48,16},{56,24},{64... | collective-permute-start | bytes 1376264 | tf_op jit(solution)/shard_map/ppermute | solution.py:26
  262.2 18.9 %collective-permute-start.5 = (bf16[256,896]{1,0:T(8,128)(2,1)S(1)}, bf16[256,896]{1,0:T(8,128)(2,1)S(1)}, u32[]{:S(2)}, u32[]{:S(2)}) collective-permute-start(bf16[256,896]{1,0:T(8,128)(2,1)S(1)} %collective-permute-done.4), channel_id=1, source_target_pairs={{0,32},{8,40},{16,48},{24,56},{32,64},{40,72},{48,80},{56,88},{64,... | collective-permute-start | bytes 1376264 | tf_op jit(solution)/shard_map/ppermute | solution.py:26
  271.3 19.7 %collective-permute-start.3 = (bf16[256,896]{1,0:T(8,128)(2,1)S(1)}, bf16[256,896]{1,0:T(8,128)(2,1)S(1)}, u32[]{:S(2)}, u32[]{:S(2)}) collective-permute-start(bf16[256,896]{1,0:T(8,128)(2,1)S(1)} %collective-permute-done.2), channel_id=1, source_target_pairs={{0,96},{8,104},{16,112},{24,120},{32,0},{40,8},{48,16},{56,24},{64... | collective-permute-start | bytes 1376264 | tf_op jit(solution)/shard_map/ppermute | solution.py:26
  271.9 19.0 %collective-permute-start.1 = (bf16[256,896]{1,0:T(8,128)(2,1)S(1)}, bf16[256,896]{1,0:T(8,128)(2,1)S(1)}, u32[]{:S(2)}, u32[]{:S(2)}) collective-permute-start(bf16[256,896]{1,0:T(8,128)(2,1)S(1)} %collective-permute-done), channel_id=1, source_target_pairs={{0,32},{8,40},{16,48},{24,56},{32,64},{40,72},{48,80},{56,88},{64,... | collective-permute-start | bytes 1376264 | tf_op jit(solution)/shard_map/ppermute | solution.py:26
  290.9 4.2 %copy-start.1 = (bf16[1,256,3584]{2,1,0:T(8,128)(2,1)S(1)}, bf16[1,256,3584]{2,1,0:T(8,128)(2,1)}, u32[]{:S(2)}) copy-start(bf16[1,256,3584]{2,1,0:T(8,128)(2,1)} %param.5) | copy-start | bytes 5505028
Sparse Core Ops, SparseCore 0:
  100.4 152.7 reduce-scatter.1

commit v3 on v2

--- a/solution.py
+++ b/solution.py
@@ -56,34 +56,56 @@
     slots = slot_numbers(routes[0], experts, capacity)
     owner = slot_owner(slots, slot_total)
     outgoing = jnp.dot(owner, tokens[0], preferred_element_type=jnp.float32).astype(jnp.bfloat16)
-    received = lax.all_to_all(
-        outgoing.reshape(experts, capacity, width),
-        "expert",
-        split_axis=0,
-        concat_axis=0,
-        tiled=True,
-    )
-    received = received.reshape(slot_total, width)
     gate_w = w_gate[0, 0]
     up_w = w_up[0, 0]
     hidden = gate_w.shape[1]
-    gate_pre = jnp.dot(received, gate_w, preferred_element_type=jnp.float32)
-    up_pre = jnp.dot(received, up_w, preferred_element_type=jnp.float32)
+    groups = lax.axis_size("dp")
+    shard = width // groups
+    parts = 4
+    part = shard // parts
+
+    def columns(value, j):
+        lead = value.shape[:-1]
+        return value.reshape(lead + (groups, parts, part))[..., j, :].reshape(lead + (groups * part,))
+
+    received = []
+    gate_pre = None
+    up_pre = None
+    for j in range(parts):
+        cols = slice(j * (width // parts), (j + 1) * (width // parts))
+        got = lax.all_to_all(
+            outgoing[:, cols].reshape(experts, capacity, width // parts),
+            "expert",
+            split_axis=0,
+            concat_axis=0,
+            tiled=True,
+        ).reshape(slot_total, width // parts)
+        received.append(got)
+        gate_part = jnp.dot(got, gate_w[cols], preferred_element_type=jnp.float32)
+        up_part = jnp.dot(got, up_w[cols], preferred_element_type=jnp.float32)
+        gate_pre = gate_part if gate_pre is None else gate_pre + gate_part
+        up_pre = up_part if up_pre is None else up_pre + up_part
     grad_gate_pre, grad_up_pre = swiglu_grads(
         hidden_grad[0, 0, 0].astype(jnp.float32), gate_pre, up_pre
     )
     both_grads = jnp.concatenate([grad_gate_pre, grad_up_pre], axis=1)
     along_slots = (((0,), (0,)), ((), ()))
-    summed = lax.psum_scatter(
-        lax.dot_general(
-            received, both_grads, along_slots, preferred_element_type=jnp.float32
-        ).astype(jnp.bfloat16),
-        "dp",
-        scatter_dimension=0,
-        tiled=True,
-    ).astype(jnp.float32)
-    grad_gate = summed[:, :hidden].astype(jnp.bfloat16)[None, None]
-    grad_up = summed[:, hidden:].astype(jnp.bfloat16)[None, None]
+    received = jnp.concatenate(received, axis=1)
+    summed = []
+    for j in range(parts):
+        summed.append(
+            lax.psum_scatter(
+                lax.dot_general(
+                    columns(received, j), both_grads, along_slots, preferred_element_type=jnp.float32
+                ).astype(jnp.bfloat16),
+                "dp",
+                scatter_dimension=0,
+                tiled=True,
+            )
+        )
+    summed = jnp.concatenate(summed, axis=0)
+    grad_gate = summed[:, :hidden][None, None]
+    grad_up = summed[:, hidden:][None, None]
 
     gather_back = owner.T
     along_hidden = (((1,), (1,)), ((), ()))

time: 303 us -> 407 us (1.34); the launches traced: 302 us -> 399 us
  local copies, waits for them, and re-layouts: 4.15 us -> 72.1 us
  matrix products: 65.4 us -> 99.7 us
  blocking collectives: 59.8 us -> 41.7 us
  starting transfers between devices: 29.7 us -> 44.3 us
    slice x1 -> x7, local copies, waits for them, and re-layouts: 0.21 us -> 39.2 us  [the longest x5 37.2 us: columns(): value.reshape(lead + (groups, parts, part))[..., j, :]]
    dot_general x3 -> x12, matrix products: 27.5 us -> 61.7 us  [the longest x4 23.4 us: shards(): lax.dot_general(columns(received, j), both_grads, along_slots, preferred_...]
    concatenate x0 -> x6, local copies, waits for them, and re-layouts: none -> 18.2 us  [the longest x5 16.2 us: shards(): received = jnp.concatenate(received, axis=1)]
    all_to_all x1 -> x2, blocking collectives: 59.8 us -> 41.7 us  [shards(): lax.all_to_all(outgoing[:, cols].reshape(experts, capacity, width // part...]
    unnamed x22 -> x34, local copies, waits for them, and re-layouts: 1.11 us -> 11.8 us
    all_to_all x0 -> x2, starting transfers between devices: none -> 9.42 us  [shards(): lax.all_to_all(outgoing[:, cols].reshape(experts, capacity, width // part...]
    ppermute x4, waiting for transfers between devices: 74.6 us -> 66.2 us  [across_sections(): hop = lax.ppermute(value, ('section', 'dp'), perm)]
    ppermute x4, starting transfers between devices: 2.93 us -> 8.19 us  [across_sections(): return lax.ppermute(hop, ('section', 'dp'), perm)]
  transfers between devices with their start and end apart: 13 -> 18, of which waited for: 8 -> 14; matrix products, arithmetic and copies ran while one was open for 13% -> 26% of each run, Pallas kernels for 0% -> 0%
where the time goes in v3:
time: 407 us; the launch traced here: 399 us
  waiting for transfers between devices  123 us (30%)
  matrix products  99.7 us (24%)
  local copies, waits for them, and re-layouts  72.1 us (18%)
  starting transfers between devices  44.3 us (11%)
  blocking collectives  41.7 us (10%)
  between operations  14.3 us (4%)
  other arithmetic  4.48 us (1%)
    ppermute x4, waiting for transfers between devices, across_sections(): hop = lax.ppermute(value, ('section', 'dp'), perm)  66.2 us
    all_to_all x2, blocking collectives, shards(): lax.all_to_all(outgoing[:, cols].reshape(experts, capacity, width // part...  41.7 us
    slice x5, local copies, waits for them, and re-layouts, columns(): value.reshape(lead + (groups, parts, part))[..., j, :]  37.2 us
    all_to_all x4, waiting for transfers between devices, shards(): lax.all_to_all(slot_grad.reshape(experts, capacity, step), 'expert', spli...  33.9 us
    dot_general x4, matrix products, shards(): lax.dot_general(columns(received, j), both_grads, along_slots, preferred_...  23.4 us
    dot_general x4, matrix products, shards(): gate_part = jnp.dot(got, gate_w[cols], preferred_element_type=jnp.float32)  20.4 us
    all_to_all x4, starting transfers between devices, shards(): lax.all_to_all(slot_grad.reshape(experts, capacity, step), 'expert', spli...  18.8 us
    dot_general x4, matrix products, shards(): up_part = jnp.dot(got, up_w[cols], preferred_element_type=jnp.float32)  17.9 us
  transfers between devices with their start and end apart: 18, of which 14 were waited for; matrix products, arithmetic and copies ran while one was open for 26% of the time, Pallas kernels for 0%

profile of v3, /device:TPU:1, one launch (start us, length us, event | category | flops | bytes accessed | tf_op | source)
XLA Modules:
  0.0 399.2 jit_solution(12959260335306811715)
XLA Ops:
  13.7 22.2 %all_to_all.40 = bf16[8,80,896]{2,1,0:T(8,128)(2,1)} all-to-all(bf16[8,80,896]{2,1,0:T(8,128)(2,1)S(1)} %bitcast.131), channel_id=1, replica_groups=mesh['section'=2,'dp'=8,'expert'=8] {'expert'}, dimensions={0} | all-to-all | bytes 2293760 | tf_op jit(solution)/shard_map/all_to_all | solution.py:76
  35.9 19.5 %all_to_all.41 = bf16[8,80,896]{2,1,0:T(8,128)(2,1)S(1)} all-to-all(bf16[8,80,896]{2,1,0:T(8,128)(2,1)S(1)} %bitcast.130), channel_id=1, replica_groups=mesh['section'=2,'dp'=8,'expert'=8] {'expert'}, dimensions={0} | all-to-all | bytes 2293760 | tf_op jit(solution)/shard_map/all_to_all | solution.py:76
  55.5 5.1 %all-to-all-start.1 = ((bf16[8,80,896]{2,1,0:T(8,128)(2,1)}), bf16[8,80,896]{2,1,0:T(8,128)(2,1)}, u32[]{:S(2)}, u32[]{:S(2)}) async-start(bf16[8,80,896]{2,1,0:T(8,128)(2,1)} %bitcast.12), calls=%async_computation.1 | async-start | bytes 2293760 | tf_op jit(solution)/shard_map/all_to_all | solution.py:76
  60.5 4.5 %fusion.11 = f32[640,1024]{1,0:T(8,128)} fusion(bf16[640,896]{1,0:T(8,128)(2,1)S(1)} %bitcast.136, bf16[1,1,3584,1024]{3,2,1,0:T(8,128)(2,1)} %param.8), kind=kOutput, calls=%fused_computation.26 | convolution fusion | flops 1174405120 | bytes 5603328 | tf_op jit(solution)/shard_map/dot_general | solution.py:84
  65.0 4.6 %fusion.7 = f32[640,1024]{1,0:T(8,128)} fusion(bf16[640,896]{1,0:T(8,128)(2,1)S(1)} %bitcast.134, bf16[1,1,3584,1024]{3,2,1,0:T(8,128)(2,1)} %param.8), kind=kOutput, calls=%fused_computation.22 | convolution fusion | flops 1174405120 | bytes 5603328 | tf_op jit(solution)/shard_map/dot_general | solution.py:84
  69.6 4.5 %fusion.23 = f32[640,1024]{1,0:T(8,128)} fusion(bf16[640,896]{1,0:T(8,128)(2,1)S(1)} %bitcast.135, bf16[1,1,3584,1024]{3,2,1,0:T(8,128)(2,1)} %param.9), kind=kOutput, calls=%fused_computation.38 | convolution fusion | flops 1174405120 | bytes 5603328 | tf_op jit(solution)/shard_map/dot_general | solution.py:85
  76.8 4.3 %all-to-all-start = ((bf16[8,80,896]{2,1,0:T(8,128)(2,1)}), bf16[8,80,896]{2,1,0:T(8,128)(2,1)S(1)}, u32[]{:S(2)}, u32[]{:S(2)}) async-start(bf16[8,80,896]{2,1,0:T(8,128)(2,1)} %bitcast.9), calls=%async_computation | async-start | bytes 2293760 | tf_op jit(solution)/shard_map/all_to_all | solution.py:76
  81.1 4.6 %fusion.27 = f32[640,1024]{1,0:T(8,128)} fusion(bf16[640,896]{1,0:T(8,128)(2,1)S(1)} %bitcast.137, bf16[1,1,3584,1024]{3,2,1,0:T(8,128)(2,1)} %param.9), kind=kOutput, calls=%fused_computation.42 | convolution fusion | flops 1174405120 | bytes 5603328 | tf_op jit(solution)/shard_map/dot_general | solution.py:85
  85.7 4.8 %fusion.15 = f32[640,1024]{1,0:T(8,128)} fusion(bf16[640,896]{1,0:T(8,128)(2,1)} %bitcast.13, bf16[1,1,3584,1024]{3,2,1,0:T(8,128)(2,1)} %param.8), kind=kOutput, calls=%fused_computation.30 | convolution fusion | flops 1174405120 | bytes 5603328 | tf_op jit(solution)/shard_map/dot_general | solution.py:84
  90.6 4.9 %fusion.31 = f32[640,1024]{1,0:T(8,128)} fusion(bf16[640,896]{1,0:T(8,128)(2,1)} %bitcast.13, bf16[1,1,3584,1024]{3,2,1,0:T(8,128)(2,1)} %param.9), kind=kOutput, calls=%fused_computation.46 | convolution fusion | flops 1174405120 | bytes 5603328 | tf_op jit(solution)/shard_map/dot_general | solution.py:85
  100.9 4.2 %concatenate.23 = bf16[640,2,4,112]{3,2,1,0:T(4,128)(2,1)S(1)} reshape(bf16[8,80,896]{2,1,0:T(8,128)(2,1)} %all-to-all-done.1) | data formatting | bytes 2293760 | tf_op jit(solution)/shard_map/concatenate | solution.py:93
  106.7 4.2 %concatenate.24 = bf16[640,2,4,112]{3,2,1,0:T(4,128)(2,1)S(1)} reshape(bf16[8,80,896]{2,1,0:T(8,128)(2,1)} %all_to_all.40) | data formatting | bytes 2293760 | tf_op jit(solution)/shard_map/concatenate | solution.py:93
  112.6 4.2 %concatenate.25 = bf16[640,2,4,112]{3,2,1,0:T(4,128)(2,1)S(1)} reshape(bf16[8,80,896]{2,1,0:T(8,128)(2,1)} %copy-done.2) | data formatting | bytes 2293760 | tf_op jit(solution)/shard_map/concatenate | solution.py:93
  118.4 17.7 %fusion.68 = (bf16[640,8,1,112]{3,2,1,0:T(2,128)(2,1)}, bf16[640,8,1,112]{3,2,1,0:T(2,128)(2,1)}, bf16[640,8,1,112]{3,2,1,0:T(2,128)(2,1)}, bf16[640,8,1,112]{3,2,1,0:T(2,128)(2,1)}) fusion(bf16[640,8,4,112]{3,2,1,0:T(4,128)(2,1)} %constant_dynamic-update-slice_fusion), kind=kLoop, calls=%fused_computation.92 | loop fusion | bytes 9175040 | tf_op jit(solution)/shard_map/slice | solution.py:69
  136.1 4.9 %copy.17 = bf16[640,8,1,112]{0,3,1,2:T(8,128)(2,1)S(1)} copy(bf16[640,8,1,112]{3,2,1,0:T(2,128)(2,1)} %get-tuple-element.6) | data formatting | bytes 2293760 | tf_op jit(solution)/shard_map/slice | solution.py:69
  141.0 6.5 %fusion.4 = (bf16[640,1024]{1,0:T(8,128)(2,1)S(1)}, f32[640,1024]{1,0:T(8,128)S(1)}) fusion(bf16[1,1,1,640,1024]{4,3,2,1,0:T(8,128)(2,1)} %param.7, f32[640,1024]{1,0:T(8,128)} %fusion.7, f32[640,1024]{1,0:T(8,128)} %fusion.11, f32[640,1024]{1,0:T(8,128)} %fusion.15, bf16[640,896]{1,0:T(8,128)(2,1)S(1)} %bitcast.132, bf16[1,1,3584,1024]{3,2,1,0:T(8,128)(2,1)} %param.8), kind=kOutput, calls=%fused_computation.11 | convolution fusion | flops 1180958720 | bytes 16089088 | tf_op jit(solution)/shard_map/dot_general | solution.py:84
  147.8 4.0 fusion.2
  152.9 4.8 %convolution_convert_fusion.4 = bf16[896,2048]{1,0:T(8,128)(2,1)} fusion(bf16[640,896]{0,1:T(8,128)(2,1)S(1)} %bitcast.138, bf16[640,1024]{1,0:T(8,128)(2,1)S(1)} %get-tuple-element.13, bf16[640,1024]{1,0:T(8,128)(2,1)S(1)} %fusion.2), kind=kOutput, calls=%fused_computation.4 | convolution fusion | flops 2355888128 | bytes 7438336 | tf_op jit(solution)/shard_map/dot_general | solution.py:98
  157.8 4.9 %copy.18 = bf16[640,8,1,112]{0,3,1,2:T(8,128)(2,1)S(1)} copy(bf16[640,8,1,112]{3,2,1,0:T(2,128)(2,1)} %get-tuple-element.5) | data formatting | bytes 2293760 | tf_op jit(solution)/shard_map/slice | solution.py:69
  162.6 6.2 %convolution_convert_fusion.3 = bf16[896,2048]{1,0:T(8,128)(2,1)} fusion(bf16[640,896]{0,1:T(8,128)(2,1)S(1)} %bitcast.139, bf16[640,1024]{1,0:T(8,128)(2,1)} %copy-done.8, bf16[640,1024]{1,0:T(8,128)(2,1)} %copy-done.13), kind=kOutput, calls=%fused_computation.3 | convolution fusion | flops 2355888128 | bytes 7438336 | tf_op jit(solution)/shard_map/dot_general | solution.py:98
  168.9 4.9 %copy.19 = bf16[640,8,1,112]{0,3,1,2:T(8,128)(2,1)S(1)} copy(bf16[640,8,1,112]{3,2,1,0:T(2,128)(2,1)} %get-tuple-element.4) | data formatting | bytes 2293760 | tf_op jit(solution)/shard_map/slice | solution.py:69
  173.8 6.2 %convolution_convert_fusion.2 = bf16[896,2048]{1,0:T(8,128)(2,1)} fusion(bf16[640,896]{0,1:T(8,128)(2,1)S(1)} %bitcast.140, bf16[640,1024]{1,0:T(8,128)(2,1)} %copy-done.8, bf16[640,1024]{1,0:T(8,128)(2,1)} %copy-done.13), kind=kOutput, calls=%fused_computation.2 | convolution fusion | flops 2355888128 | bytes 7438336 | tf_op jit(solution)/shard_map/dot_general | solution.py:98
  180.1 4.9 %copy.20 = bf16[640,8,1,112]{0,3,1,2:T(8,128)(2,1)S(1)} copy(bf16[640,8,1,112]{3,2,1,0:T(2,128)(2,1)} %get-tuple-element.3) | data formatting | bytes 2293760 | tf_op jit(solution)/shard_map/slice | solution.py:69
  185.0 6.2 %convolution_convert_fusion.1 = bf16[896,2048]{1,0:T(8,128)(2,1)} fusion(bf16[640,896]{0,1:T(8,128)(2,1)S(1)} %bitcast.141, bf16[640,1024]{1,0:T(8,128)(2,1)} %copy-done.8, bf16[640,1024]{1,0:T(8,128)(2,1)} %copy-done.13), kind=kOutput, calls=%fused_computation.1 | convolution fusion | flops 2355888128 | bytes 7438336 | tf_op jit(solution)/shard_map/dot_general | solution.py:98
  191.2 3.6 fusion.17
  194.8 4.1 %add_convert_fusion.3 = bf16[640,896]{1,0:T(8,128)(2,1)} fusion(f32[640,896]{1,0:T(8,128)S(1)} %fusion.17, bf16[640,1024]{1,0:T(8,128)(2,1)S(1)} %copy-done.9, bf16[1,1,3584,1024]{3,2,1,0:T(8,128)(2,1)} %param.9), kind=kOutput, calls=%fused_computation.18 | convolution fusion | flops 1175552000 | bytes 6586368 | tf_op jit(solution)/shard_map/dot_general | solution.py:119
  198.9 4.3 %all-to-all-start.4 = ((bf16[8,80,896]{2,1,0:T(8,128)(2,1)}), bf16[8,80,896]{2,1,0:T(8,128)(2,1)S(1)}, u32[]{:S(2)}, u32[]{:S(2)}) async-start(bf16[8,80,896]{2,1,0:T(8,128)(2,1)} %bitcast.26), calls=%async_computation.4 | async-start | bytes 2293760 | tf_op jit(solution)/shard_map/all_to_all | solution.py:121
  203.3 3.6 fusion.13
  206.9 4.2 %add_convert_fusion.2 = bf16[640,896]{1,0:T(8,128)(2,1)} fusion(f32[640,896]{1,0:T(8,128)S(1)} %fusion.13, bf16[640,1024]{1,0:T(8,128)(2,1)S(1)} %copy-done.10, bf16[1,1,3584,1024]{3,2,1,0:T(8,128)(2,1)} %param.9), kind=kOutput, calls=%fused_computation.17 | convolution fusion | flops 1175552000 | bytes 6586368 | tf_op jit(solution)/shard_map/dot_general | solution.py:119
  211.1 8.4 %all-to-all-done.4 = bf16[8,80,896]{2,1,0:T(8,128)(2,1)S(1)} async-done(((bf16[8,80,896]{2,1,0:T(8,128)(2,1)}), bf16[8,80,896]{2,1,0:T(8,128)(2,1)S(1)}, u32[]{:S(2)}, u32[]{:S(2)}) %all-to-all-start.4) | async-done | bytes 1146912 | tf_op jit(solution)/shard_map/all_to_all | solution.py:121
  219.4 4.6 %all-to-all-start.5 = ((bf16[8,80,896]{2,1,0:T(8,128)(2,1)}), bf16[8,80,896]{2,1,0:T(8,128)(2,1)S(1)}, u32[]{:S(2)}, u32[]{:S(2)}) async-start(bf16[8,80,896]{2,1,0:T(8,128)(2,1)} %bitcast.146), calls=%async_computation.5 | async-start | bytes 2293760 | tf_op jit(solution)/shard_map/all_to_all | solution.py:121
  224.0 3.6 fusion.9
  227.6 4.2 %add_convert_fusion.1 = bf16[640,896]{1,0:T(8,128)(2,1)} fusion(f32[640,896]{1,0:T(8,128)S(1)} %fusion.9, bf16[640,1024]{1,0:T(8,128)(2,1)S(1)} %copy-done.11, bf16[1,1,3584,1024]{3,2,1,0:T(8,128)(2,1)} %param.9), kind=kOutput, calls=%fused_computation.16 | convolution fusion | flops 1175552000 | bytes 6586368 | tf_op jit(solution)/shard_map/dot_general | solution.py:119
  231.8 8.5 %all-to-all-done.5 = bf16[8,80,896]{2,1,0:T(8,128)(2,1)S(1)} async-done(((bf16[8,80,896]{2,1,0:T(8,128)(2,1)}), bf16[8,80,896]{2,1,0:T(8,128)(2,1)S(1)}, u32[]{:S(2)}, u32[]{:S(2)}) %all-to-all-start.5) | async-done | bytes 1146912 | tf_op jit(solution)/shard_map/all_to_all | solution.py:121
  240.3 4.9 %all-to-all-start.6 = ((bf16[8,80,896]{2,1,0:T(8,128)(2,1)}), bf16[8,80,896]{2,1,0:T(8,128)(2,1)}, u32[]{:S(2)}, u32[]{:S(2)}) async-start(bf16[8,80,896]{2,1,0:T(8,128)(2,1)} %bitcast.145), calls=%async_computation.6 | async-start | bytes 2293760 | tf_op jit(solution)/shard_map/all_to_all | solution.py:121
  245.2 3.6 fusion.5
  248.8 4.2 %add_convert_fusion = bf16[640,896]{1,0:T(8,128)(2,1)} fusion(f32[640,896]{1,0:T(8,128)S(1)} %fusion.5, bf16[640,1024]{1,0:T(8,128)(2,1)S(1)} %copy-done.12, bf16[1,1,3584,1024]{3,2,1,0:T(8,128)(2,1)} %param.9), kind=kOutput, calls=%fused_computation.15 | convolution fusion | flops 1175552000 | bytes 6586368 | tf_op jit(solution)/shard_map/dot_general | solution.py:119
  252.9 8.5 %all-to-all-done.6 = bf16[8,80,896]{2,1,0:T(8,128)(2,1)} async-done(((bf16[8,80,896]{2,1,0:T(8,128)(2,1)}), bf16[8,80,896]{2,1,0:T(8,128)(2,1)}, u32[]{:S(2)}, u32[]{:S(2)}) %all-to-all-start.6) | async-done | bytes 1146912 | tf_op jit(solution)/shard_map/all_to_all | solution.py:121
  261.4 5.0 %all-to-all-start.7 = ((bf16[8,80,896]{2,1,0:T(8,128)(2,1)}), bf16[8,80,896]{2,1,0:T(8,128)(2,1)}, u32[]{:S(2)}, u32[]{:S(2)}) async-start(bf16[8,80,896]{2,1,0:T(8,128)(2,1)} %bitcast.144), calls=%async_computation.7 | async-start | bytes 2293760 | tf_op jit(solution)/shard_map/all_to_all | solution.py:121
  274.2 8.5 %all-to-all-done.7 = bf16[8,80,896]{2,1,0:T(8,128)(2,1)} async-done(((bf16[8,80,896]{2,1,0:T(8,128)(2,1)}), bf16[8,80,896]{2,1,0:T(8,128)(2,1)}, u32[]{:S(2)}, u32[]{:S(2)}) %all-to-all-start.7) | async-done | bytes 1146912 | tf_op jit(solution)/shard_map/all_to_all | solution.py:121
  284.6 3.8 collective-permute-start.6
  288.4 25.6 %collective-permute-done = bf16[256,896]{1,0:T(8,128)(2,1)} collective-permute-done((bf16[256,896]{1,0:T(8,128)(2,1)}, bf16[256,896]{1,0:T(8,128)(2,1)}, u32[]{:S(2)}, u32[]{:S(2)}) %collective-permute-start) | collective-permute-done | bytes 458784 | tf_op jit(solution)/shard_map/ppermute | solution.py:25
  318.7 39.3 %collective-permute-done.4 = bf16[256,896]{1,0:T(8,128)(2,1)S(1)} collective-permute-done((bf16[256,896]{1,0:T(8,128)(2,1)S(1)}, bf16[256,896]{1,0:T(8,128)(2,1)S(1)}, u32[]{:S(2)}, u32[]{:S(2)}) %collective-permute-start.4) | collective-permute-done | bytes 458784 | tf_op jit(solution)/shard_map/ppermute | solution.py:25
  362.9 5.2 %collective-permute-done.1 = bf16[256,896]{1,0:T(8,128)(2,1)S(1)} collective-permute-done((bf16[256,896]{1,0:T(8,128)(2,1)}, bf16[256,896]{1,0:T(8,128)(2,1)S(1)}, u32[]{:S(2)}, u32[]{:S(2)}) %collective-permute-start.1) | collective-permute-done | bytes 458784 | tf_op jit(solution)/shard_map/ppermute | solution.py:26
  368.1 2.8 collective-permute-done.3
  370.9 6.9 %collective-permute-done.5 = bf16[256,896]{1,0:T(8,128)(2,1)S(1)} collective-permute-done((bf16[256,896]{1,0:T(8,128)(2,1)S(1)}, bf16[256,896]{1,0:T(8,128)(2,1)S(1)}, u32[]{:S(2)}, u32[]{:S(2)}) %collective-permute-start.5) | collective-permute-done | bytes 458784 | tf_op jit(solution)/shard_map/ppermute | solution.py:26
  377.8 2.9 collective-permute-done.7
  389.6 2.8 slice_bitcast_fusion
  (76 shorter events, 49.1 us)
Async XLA Ops:
  7.2 3.4 copy-start
  55.4 14.2 %copy-start.2 = (bf16[8,80,896]{2,1,0:T(8,128)(2,1)}, bf16[8,80,896]{2,1,0:T(8,128)(2,1)S(1)}, u32[]{:S(2)}) copy-start(bf16[8,80,896]{2,1,0:T(8,128)(2,1)S(1)} %all_to_all.41) | copy-start | bytes 3440644
  55.4 5.1 %copy-start.3 = (bf16[8,80,896]{2,1,0:T(8,128)(2,1)S(1)}, bf16[8,80,896]{2,1,0:T(8,128)(2,1)}, u32[]{:S(2)}) copy-start(bf16[8,80,896]{2,1,0:T(8,128)(2,1)} %all_to_all.40) | copy-start | bytes 3440644
  55.5 21.4 %all-to-all-start.1 = ((bf16[8,80,896]{2,1,0:T(8,128)(2,1)}), bf16[8,80,896]{2,1,0:T(8,128)(2,1)}, u32[]{:S(2)}, u32[]{:S(2)}) async-start(bf16[8,80,896]{2,1,0:T(8,128)(2,1)} %bitcast.12), calls=%async_computation.1 | async-start | bytes 2293760 | tf_op jit(solution)/shard_map/all_to_all | solution.py:76
  76.8 20.5 %all-to-all-start = ((bf16[8,80,896]{2,1,0:T(8,128)(2,1)}), bf16[8,80,896]{2,1,0:T(8,128)(2,1)S(1)}, u32[]{:S(2)}, u32[]{:S(2)}) async-start(bf16[8,80,896]{2,1,0:T(8,128)(2,1)} %bitcast.9), calls=%async_computation | async-start | bytes 2293760 | tf_op jit(solution)/shard_map/all_to_all | solution.py:76
  81.1 301.0 %reduce-scatter.5.cloned.1.call-start = ((), (), s32[]{:S(2)}) async-start(), calls=%async_computation.12 | async-start | bytes 4128768 | tf_op jit(solution)/shard_map/reduce_scatter | solution.py:97
  140.9 6.5 %copy-start.4 = (bf16[1,1,1,640,1024]{4,3,2,1,0:T(8,128)(2,1)S(1)}, bf16[1,1,1,640,1024]{4,3,2,1,0:T(8,128)(2,1)}, u32[]{:S(2)}) copy-start(bf16[1,1,1,640,1024]{4,3,2,1,0:T(8,128)(2,1)} %param.7) | copy-start | bytes 3932164
  140.9 6.5 %copy-start.5 = (f32[640,1024]{1,0:T(8,128)S(1)}, f32[640,1024]{1,0:T(8,128)}, u32[]{:S(2)}) copy-start(f32[640,1024]{1,0:T(8,128)} %fusion.23) | copy-start | bytes 7864324
  141.0 6.5 %copy-start.6 = (f32[640,1024]{1,0:T(8,128)S(1)}, f32[640,1024]{1,0:T(8,128)}, u32[]{:S(2)}) copy-start(f32[640,1024]{1,0:T(8,128)} %fusion.27) | copy-start | bytes 7864324
  141.0 6.9 %copy-start.7 = (f32[640,1024]{1,0:T(8,128)S(1)}, f32[640,1024]{1,0:T(8,128)}, u32[]{:S(2)}) copy-start(f32[640,1024]{1,0:T(8,128)} %fusion.31) | copy-start | bytes 7864324
  147.4 4.4 %copy-start.8 = (bf16[640,1024]{1,0:T(8,128)(2,1)}, bf16[640,1024]{1,0:T(8,128)(2,1)S(1)}, u32[]{:S(2)}) copy-start(bf16[640,1024]{1,0:T(8,128)(2,1)S(1)} %get-tuple-element.13) | copy-start | bytes 3932164
  151.8 1.1 copy-start.13
  157.7 226.2 %reduce-scatter.7.cloned.1.call-start = ((), (), s32[]{:S(2)}) async-start(), calls=%async_computation.13 | async-start | bytes 4128768 | tf_op jit(solution)/shard_map/reduce_scatter | solution.py:97
  168.8 217.0 %reduce-scatter.9.cloned.1.call-start = ((), (), s32[]{:S(2)}) async-start(), calls=%async_computation.14 | async-start | bytes 4128768 | tf_op jit(solution)/shard_map/reduce_scatter | solution.py:97
  180.0 207.6 %reduce-scatter.11.cloned.1.call-start = ((), (), s32[]{:S(2)}) async-start(), calls=%async_computation.15 | async-start | bytes 4128768 | tf_op jit(solution)/shard_map/reduce_scatter | solution.py:97
  191.2 3.6 copy-start.9
  198.9 20.5 %all-to-all-start.4 = ((bf16[8,80,896]{2,1,0:T(8,128)(2,1)}), bf16[8,80,896]{2,1,0:T(8,128)(2,1)S(1)}, u32[]{:S(2)}, u32[]{:S(2)}) async-start(bf16[8,80,896]{2,1,0:T(8,128)(2,1)} %bitcast.26), calls=%async_computation.4 | async-start | bytes 2293760 | tf_op jit(solution)/shard_map/all_to_all | solution.py:121
  203.3 3.6 copy-start.10
  219.4 20.8 %all-to-all-start.5 = ((bf16[8,80,896]{2,1,0:T(8,128)(2,1)}), bf16[8,80,896]{2,1,0:T(8,128)(2,1)S(1)}, u32[]{:S(2)}, u32[]{:S(2)}) async-start(bf16[8,80,896]{2,1,0:T(8,128)(2,1)} %bitcast.146), calls=%async_computation.5 | async-start | bytes 2293760 | tf_op jit(solution)/shard_map/all_to_all | solution.py:121
  224.0 3.6 copy-start.11
  240.3 21.2 %all-to-all-start.6 = ((bf16[8,80,896]{2,1,0:T(8,128)(2,1)}), bf16[8,80,896]{2,1,0:T(8,128)(2,1)}, u32[]{:S(2)}, u32[]{:S(2)}) async-start(bf16[8,80,896]{2,1,0:T(8,128)(2,1)} %bitcast.145), calls=%async_computation.6 | async-start | bytes 2293760 | tf_op jit(solution)/shard_map/all_to_all | solution.py:121
  245.2 3.6 copy-start.12
  261.4 21.3 %all-to-all-start.7 = ((bf16[8,80,896]{2,1,0:T(8,128)(2,1)}), bf16[8,80,896]{2,1,0:T(8,128)(2,1)}, u32[]{:S(2)}, u32[]{:S(2)}) async-start(bf16[8,80,896]{2,1,0:T(8,128)(2,1)} %bitcast.144), calls=%async_computation.7 | async-start | bytes 2293760 | tf_op jit(solution)/shard_map/all_to_all | solution.py:121
  267.8 46.2 %collective-permute-start = (bf16[256,896]{1,0:T(8,128)(2,1)}, bf16[256,896]{1,0:T(8,128)(2,1)}, u32[]{:S(2)}, u32[]{:S(2)}) collective-permute-start(bf16[256,896]{1,0:T(8,128)(2,1)} %convolution_convert_fusion.8), channel_id=1, source_target_pairs={{0,32},{8,40},{16,48},{24,56},{32,64},{40,72},{48,80},{56,88},{64,... | collective-permute-start | bytes 1376264 | tf_op jit(solution)/shard_map/ppermute | solution.py:25
  270.1 46.8 %collective-permute-start.2 = (bf16[256,896]{1,0:T(8,128)(2,1)S(1)}, bf16[256,896]{1,0:T(8,128)(2,1)S(1)}, u32[]{:S(2)}, u32[]{:S(2)}) collective-permute-start(bf16[256,896]{1,0:T(8,128)(2,1)S(1)} %convolution_convert_fusion.7), channel_id=1, source_target_pairs={{0,96},{8,104},{16,112},{24,120},{32,0},{40,8},{48,16},{56,24},{64... | collective-permute-start | bytes 1376264 | tf_op jit(solution)/shard_map/ppermute | solution.py:25
  274.1 83.9 %collective-permute-start.4 = (bf16[256,896]{1,0:T(8,128)(2,1)S(1)}, bf16[256,896]{1,0:T(8,128)(2,1)S(1)}, u32[]{:S(2)}, u32[]{:S(2)}) collective-permute-start(bf16[256,896]{1,0:T(8,128)(2,1)S(1)} %convolution_convert_fusion.6), channel_id=1, source_target_pairs={{0,32},{8,40},{16,48},{24,56},{32,64},{40,72},{48,80},{56,88},{64,... | collective-permute-start | bytes 1376264 | tf_op jit(solution)/shard_map/ppermute | solution.py:25
  284.6 76.5 %collective-permute-start.6 = (bf16[256,896]{1,0:T(8,128)(2,1)S(1)}, bf16[256,896]{1,0:T(8,128)(2,1)S(1)}, u32[]{:S(2)}, u32[]{:S(2)}) collective-permute-start(bf16[256,896]{1,0:T(8,128)(2,1)S(1)} %convolution_convert_fusion.5), channel_id=1, source_target_pairs={{0,96},{8,104},{16,112},{24,120},{32,0},{40,8},{48,16},{56,24},{64... | collective-permute-start | bytes 1376264 | tf_op jit(solution)/shard_map/ppermute | solution.py:25
  314.0 54.1 %collective-permute-start.1 = (bf16[256,896]{1,0:T(8,128)(2,1)}, bf16[256,896]{1,0:T(8,128)(2,1)S(1)}, u32[]{:S(2)}, u32[]{:S(2)}) collective-permute-start(bf16[256,896]{1,0:T(8,128)(2,1)} %collective-permute-done), channel_id=1, source_target_pairs={{0,32},{8,40},{16,48},{24,56},{32,64},{40,72},{48,80},{56,88},{64,... | collective-permute-start | bytes 1376264 | tf_op jit(solution)/shard_map/ppermute | solution.py:26
  316.8 54.1 %collective-permute-start.3 = (bf16[256,896]{1,0:T(8,128)(2,1)S(1)}, bf16[256,896]{1,0:T(8,128)(2,1)S(1)}, u32[]{:S(2)}, u32[]{:S(2)}) collective-permute-start(bf16[256,896]{1,0:T(8,128)(2,1)S(1)} %collective-permute-done.2), channel_id=1, source_target_pairs={{0,96},{8,104},{16,112},{24,120},{32,0},{40,8},{48,16},{56,24},{64... | collective-permute-start | bytes 1376264 | tf_op jit(solution)/shard_map/ppermute | solution.py:26
  358.0 19.8 %collective-permute-start.5 = (bf16[256,896]{1,0:T(8,128)(2,1)S(1)}, bf16[256,896]{1,0:T(8,128)(2,1)S(1)}, u32[]{:S(2)}, u32[]{:S(2)}) collective-permute-start(bf16[256,896]{1,0:T(8,128)(2,1)S(1)} %collective-permute-done.4), channel_id=1, source_target_pairs={{0,32},{8,40},{16,48},{24,56},{32,64},{40,72},{48,80},{56,88},{64,... | collective-permute-start | bytes 1376264 | tf_op jit(solution)/shard_map/ppermute | solution.py:26
  361.1 19.7 %collective-permute-start.7 = (bf16[256,896]{1,0:T(8,128)(2,1)S(1)}, bf16[256,896]{1,0:T(8,128)(2,1)S(1)}, u32[]{:S(2)}, u32[]{:S(2)}) collective-permute-start(bf16[256,896]{1,0:T(8,128)(2,1)S(1)} %collective-permute-done.6), channel_id=1, source_target_pairs={{0,96},{8,104},{16,112},{24,120},{32,0},{40,8},{48,16},{56,24},{64... | collective-permute-start | bytes 1376264 | tf_op jit(solution)/shard_map/ppermute | solution.py:26
  387.6 4.8 %copy-start.1 = (bf16[1,256,3584]{2,1,0:T(8,128)(2,1)S(1)}, bf16[1,256,3584]{2,1,0:T(8,128)(2,1)}, u32[]{:S(2)}) copy-start(bf16[1,256,3584]{2,1,0:T(8,128)(2,1)} %param.5) | copy-start | bytes 5505028
Sparse Core Ops, SparseCore 0:
  157.8 47.4 reduce-scatter.4
  207.7 48.3 reduce-scatter.6
  258.5 47.6 reduce-scatter.8
  308.5 48.6 reduce-scatter.10
